TPU v7x, 256 devices: a whole 4x4x8 slice. The times are simulated.
256 devices in a mesh: feat: 64 (over y, x, z_hi), mp: 4 (over z_lo, core).
Axes of the slice: x: 4, y: 4, z: 8 (z_hi: 4, z_lo: 2; z = z_hi * 2 + z_lo), core: 2. Of those that a mesh axis runs over, the one named last changes fastest.
Arguments:
- acts_in: bfloat16 [3, 512, 3584], P(None, 'feat', 'mp'), may hold values from -6 to 6
- targets: bfloat16 [3, 512, 3584], P(None, 'feat', 'mp'), may hold values from -6 to 6
- enc_weight: bfloat16 [3, 3584, 16384], P(None, 'mp', 'feat'), may hold values from -0.09375 to 0.09375
- enc_bias: float32 [3, 16384], P(None, 'feat'), may hold values from -3 to 3
- dec_weight: bfloat16 [6, 16384, 3584], P(None, 'feat', 'mp'), may hold values from -0.046875 to 0.046875
- dec_bias: float32 [3, 3584], P(None, 'mp'), may hold values from -3 to 3
Outputs:
- residual_error: bfloat16 [3, 512, 3584], P(None, 'feat', 'mp')
- grad_enc: bfloat16 [3, 3584, 16384], P(None, 'mp', 'feat')
- grad_dec: bfloat16 [6, 16384, 3584], P(None, 'feat', 'mp')
- grad_enc_bias: float32 [3, 16384], P(None, 'feat')
All inputs are finite; a program needn't handle non-finite values.
Results may differ from a plain program's by a relative error of at most 0.014.
Values may be sent and summed in bfloat16 or wider, within the bound.
No kernel may reach another device: no remote copies, remote signals or barrier semaphores. Data moves between devices by JAX's collectives and lax.ppermute only.
A program may use at most 64 MiB of HBM per device.

v0:
```python
import math

import jax
import jax.numpy as jnp
from jax import lax
from jax.sharding import Mesh, PartitionSpec as P


BF16 = jnp.bfloat16
F32 = jnp.float32
FEAT = ("y", "x", "zh")
MP = ("zl", "core")
RING = 4
ORDER = (0, 2, 1, 3)


def pair_index(source, target, layers):
    return source * (2 * layers - source + 1) // 2 + target - source


def shift(value, stage, by):
    if stage == "zh":
        return lax.ppermute(value, "zh", [(i, (i + by) % RING) for i in range(RING)])
    pairs = []
    for y in range(RING):
        for x in range(RING):
            for core in range(2):
                if (stage == "first") == (core == 0):
                    to = (y, (x + by) % RING)
                else:
                    to = ((y + by) % RING, x)
                pairs.append(((y * RING + x) * 2 + core, (to[0] * RING + to[1]) * 2 + core))
    return lax.ppermute(value, ("y", "x", "core"), pairs)


def swap(value, axis):
    return lax.ppermute(value, axis, [(0, 1), (1, 0)])


def flip(value):
    lead, rows, width = value.shape
    return value.reshape(lead, RING, RING, rows // RING**2, width).swapaxes(1, 2).reshape(value.shape)


def core_add(value):
    lead, rows, width = value.shape
    blocks = value.reshape(lead, RING**2, 2, rows // (2 * RING**2), width)
    me = lax.axis_index("core")
    mine = lax.dynamic_index_in_dim(blocks, me, 2, keepdims=False).reshape(lead, rows // 2, width)
    theirs = lax.dynamic_index_in_dim(blocks, 1 - me, 2, keepdims=False).reshape(lead, rows // 2, width)
    return mine.astype(F32) + flip(swap(theirs, "core")).astype(F32)


def core_join(value):
    lead, rows, width = value.shape
    got = flip(swap(value, "core"))
    first = lax.axis_index("core") == 0
    split = (lead, RING**2, 1, rows // RING**2, width)
    halves = [jnp.where(first, value, got).reshape(split), jnp.where(first, got, value).reshape(split)]
    return jnp.concatenate(halves, axis=2).reshape(lead, 2 * rows, width)


def chip_add(value):
    rows = value.shape[1] // 2
    me = lax.axis_index("zl")
    mine = lax.dynamic_slice_in_dim(value, me * rows, rows, 1)
    theirs = lax.dynamic_slice_in_dim(value, (1 - me) * rows, rows, 1)
    return mine.astype(F32) + swap(theirs, "zl").astype(F32)


def chip_join(value):
    got = swap(value, "zl")
    first = lax.axis_index("zl") == 0
    return jnp.concatenate([jnp.where(first, value, got), jnp.where(first, got, value)], axis=1)


def spread(value, stage):
    slots = {s: shift(value, stage, s) for s in ORDER[1:]}
    return jnp.concatenate([value] + [slots[s] for s in ORDER[1:]], axis=1)


def fold(value, stage):
    n = value.shape[1] // RING
    total = value[:, :n].astype(F32)
    for i in (2, 3, 1):
        piece = value[:, i * n : (i + 1) * n].astype(BF16)
        total = total + shift(piece, stage, -ORDER[i]).astype(F32)
    return total


def gather_zh(value):
    copies = jnp.broadcast_to(value[None], (RING,) + value.shape)
    got = lax.optimization_barrier(lax.all_to_all(copies, "zh", split_axis=0, concat_axis=0, tiled=True))
    return jnp.moveaxis(got, 0, 1).reshape(value.shape[0], -1, value.shape[2])


def fold_all(value):
    total = value.astype(F32)
    for s in ORDER[1:]:
        total = total + shift(value, "zh", s).astype(F32)
    return total


def spread_wide(value):
    n = value.shape[1]
    slots = {s: shift(value, "second", s) for s in ORDER[1:]}
    full = jnp.zeros((value.shape[0], RING * n, value.shape[2]), value.dtype)
    full = lax.dynamic_update_slice_in_dim(full, value, 0, 1)
    for i in range(1, RING):
        full = lax.dynamic_update_slice_in_dim(full, slots[ORDER[i]], i * n, 1)
    return full


def on_device(acts_in, targets, enc_weight, enc_bias, dec_weight, dec_bias):
    layers = enc_weight.shape[0]
    near = gather_zh(jnp.concatenate([acts_in, targets], axis=0))
    targets_near = near[layers:]
    acts = spread_wide(lax.optimization_barrier(spread(near[:layers], "first")))
    loss_scale = 1.0 / math.sqrt(acts.shape[1])

    partial = jnp.einsum("ltd,ldf->ltf", acts, enc_weight, preferred_element_type=F32)
    pre_own = chip_add(core_add(partial)) + enc_bias[:, None, :]
    half_feature = chip_join(jnp.maximum(pre_own, 0.0).astype(BF16))
    feature = core_join(half_feature)

    totals = []
    for target in range(layers):
        total = 0.0
        for source in range(target + 1):
            total = total + jnp.dot(
                feature[source], dec_weight[pair_index(source, target, layers)], preferred_element_type=F32
            )
        totals.append(total.astype(BF16))
    part = fold(lax.optimization_barrier(fold(jnp.stack(totals), "second")), "first")
    recon = fold_all(part.astype(BF16))
    near = (recon + dec_bias[:, None, :] - targets_near.astype(F32)).astype(BF16)
    rows = targets.shape[1]
    errors = lax.dynamic_slice_in_dim(near, lax.axis_index("zh") * rows, rows, 1)
    near = near + swap(near[:, :1, :1], "core") * jnp.zeros((), BF16)
    err_first = lax.optimization_barrier(spread(near, "first"))
    late = spread_wide(err_first[1:])
    early = spread_wide(err_first[:1])
    err_all = [early[0]] + [late[i] for i in range(layers - 1)]

    grad_dec, grad_pre = {}, []
    for batch in (range(1, layers), range(1)):
        grad_act = []
        for source in batch:
            total = 0.0
            for target in range(source, layers):
                pair = pair_index(source, target, layers)
                total = total + jnp.einsum("td,fd->tf", err_all[target], dec_weight[pair], preferred_element_type=F32)
                prod = jnp.einsum("tf,td->fd", feature[source], err_all[target], preferred_element_type=F32)
                grad_dec[pair] = (prod * loss_scale).astype(BF16)
            grad_act.append((total * loss_scale).astype(BF16))
        half = core_add(jnp.stack(grad_act)).astype(BF16)
        other = swap(half, "zl")
        summed = half.astype(F32) + other.astype(F32)
        active = half_feature[batch.start : batch.stop] > 0.0
        grad_pre.append(core_join(jnp.where(active, summed, 0.0).astype(BF16)))
    grad_pre = jnp.concatenate(grad_pre[::-1], axis=0)
    grad_enc = jnp.einsum("ltd,ltf->ldf", acts, grad_pre, preferred_element_type=F32).astype(BF16)
    grad_bias = jnp.sum(grad_pre.astype(F32), axis=1)
    return (errors, grad_enc, jnp.stack([grad_dec[pair] for pair in range(len(grad_dec))]), grad_bias)


def solution(mesh):
    fine = Mesh(mesh.devices.reshape(RING, RING, RING, 2, 2), FEAT + MP)
    return jax.shard_map(
        on_device,
        mesh=fine,
        in_specs=(
            P(None, FEAT, MP),
            P(None, FEAT, MP),
            P(None, MP, FEAT),
            P(None, FEAT),
            P(None, FEAT, MP),
            P(None, MP),
        ),
        out_specs=(
            P(None, FEAT, MP),
            P(None, MP, FEAT),
            P(None, FEAT, MP),
            P(None, FEAT),
        ),
        check_vma=False,
    )
```

profile of v0, /device:TPU:1, one launch (start us, length us, event | category | flops | bytes accessed | tf_op | source)
XLA Modules:
  0.0 197.6 jit_solution(4821609124924689254)
XLA Ops:
  1.6 19.8 %all_to_all.5 = bf16[4,6,8,896]{3,2,1,0:T(8,128)(2,1)S(1)} all-to-all(bf16[4,6,8,896]{3,2,1,0:T(8,128)(2,1)S(1)} %broadcast_in_dim.8), channel_id=1, replica_groups=mesh['y'=4,'x'=4,'zh'=4,'zl'=2,'core'=2] {'zh'}, dimensions={0} | all-to-all | bytes 688128 | tf_op jit(solution)/shard_map/all_to_all | solution.py:93
  21.5 2.8 %collective-permute-start.2 = (bf16[3,32,896]{2,1,0:T(8,128)(2,1)S(1)}, bf16[3,32,896]{2,1,0:T(8,128)(2,1)S(1)}, u32[]{:S(2)}, u32[]{:S(2)}) collective-permute-start(bf16[3,32,896]{2,1,0:T(8,128)(2,1)S(1)} %slice_bitcast_fusion.13), channel_id=1, source_target_pairs={{0,48},{1,193},{16,0},{17,209},{32,16},{33,225},{48,32},{49,241},{... | collective-permute-start | bytes 516104 | tf_op jit(solution)/shard_map/ppermute | solution.py:33
  26.6 5.3 %collective-permute-done.1 = bf16[3,32,896]{2,1,0:T(8,128)(2,1)S(1)} collective-permute-done((bf16[3,32,896]{2,1,0:T(8,128)(2,1)S(1)}, bf16[3,32,896]{2,1,0:T(8,128)(2,1)S(1)}, u32[]{:S(2)}, u32[]{:S(2)}) %collective-permute-start.1) | collective-permute-done | bytes 172064 | tf_op jit(solution)/shard_map/ppermute | solution.py:33
  32.0 2.7 %collective-permute-start.3 = (bf16[3,128,896]{2,1,0:T(8,128)(2,1)S(1)}, bf16[3,128,896]{2,1,0:T(8,128)(2,1)}, u32[]{:S(2)}, u32[]{:S(2)}) collective-permute-start(bf16[3,128,896]{2,1,0:T(8,128)(2,1)S(1)} %pad_maximum_fusion.2), channel_id=1, source_target_pairs={{0,128},{1,33},{16,144},{17,49},{32,160},{33,1},{48,176},{49,17},{... | collective-permute-start | bytes 2064392 | tf_op jit(solution)/shard_map/ppermute | solution.py:33
  37.5 6.0 %collective-permute-done.3 = bf16[3,128,896]{2,1,0:T(8,128)(2,1)} collective-permute-done((bf16[3,128,896]{2,1,0:T(8,128)(2,1)S(1)}, bf16[3,128,896]{2,1,0:T(8,128)(2,1)}, u32[]{:S(2)}, u32[]{:S(2)}) %collective-permute-start.3) | collective-permute-done | bytes 688160 | tf_op jit(solution)/shard_map/ppermute | solution.py:33
  44.7 6.4 %collective-permute-done.4 = bf16[3,128,896]{2,1,0:T(8,128)(2,1)} collective-permute-done((bf16[3,128,896]{2,1,0:T(8,128)(2,1)S(1)}, bf16[3,128,896]{2,1,0:T(8,128)(2,1)}, u32[]{:S(2)}, u32[]{:S(2)}) %collective-permute-start.4) | collective-permute-done | bytes 688160 | tf_op jit(solution)/shard_map/ppermute | solution.py:33
  55.0 12.5 %collective-permute-start.6 = (f32[3,256,256]{2,1,0:T(8,128)}, f32[3,256,256]{2,1,0:T(8,128)S(1)}, u32[]{:S(2)}, u32[]{:S(2)}) collective-permute-start(f32[3,256,256]{2,1,0:T(8,128)} %bitcast.4), channel_id=1, source_target_pairs={{0,1},{1,0},{2,3},{3,2},{4,5},{5,4},{6,7},{7,6},{8,9},{9,8},{10,11... | collective-permute-start | bytes 2359304 | tf_op jit(solution)/shard_map/ppermute | solution.py:37
  71.3 9.7 %collective-permute-done.7 = f32[3,128,256]{2,1,0:T(8,128)S(1)} collective-permute-done((f32[3,128,256]{2,1,0:T(8,128)}, f32[3,128,256]{2,1,0:T(8,128)S(1)}, u32[]{:S(2)}, u32[]{:S(2)}) %collective-permute-start.7) | collective-permute-done | bytes 393248 | tf_op jit(solution)/shard_map/ppermute | solution.py:37
  82.0 4.5 %collective-permute-done.8 = bf16[3,128,256]{2,1,0:T(8,128)(2,1)S(1)} collective-permute-done((bf16[3,128,256]{2,1,0:T(8,128)(2,1)S(1)}, bf16[3,128,256]{2,1,0:T(8,128)(2,1)S(1)}, u32[]{:S(2)}, u32[]{:S(2)}) %collective-permute-start.8) | collective-permute-done | bytes 196640 | tf_op jit(solution)/shard_map/ppermute | solution.py:37
  95.5 2.7 %collective-permute-start.10 = (bf16[3,128,896]{2,1,0:T(8,128)(2,1)S(1)}, bf16[3,128,896]{2,1,0:T(8,128)(2,1)S(1)}, u32[]{:S(2)}, u32[]{:S(2)}) collective-permute-start(bf16[3,128,896]{2,1,0:T(8,128)(2,1)S(1)} %get-tuple-element.4), channel_id=1, source_target_pairs={{0,192},{1,49},{16,208},{17,1},{32,224},{33,17},{48,240},{49,33},{... | collective-permute-start | bytes 2064392 | tf_op jit(solution)/shard_map/ppermute | solution.py:33
  98.2 8.7 %collective-permute-done.12 = bf16[3,128,896]{2,1,0:T(8,128)(2,1)S(1)} collective-permute-done((bf16[3,128,896]{2,1,0:T(8,128)(2,1)S(1)}, bf16[3,128,896]{2,1,0:T(8,128)(2,1)S(1)}, u32[]{:S(2)}, u32[]{:S(2)}) %collective-permute-start.12) | collective-permute-done | bytes 688160 | tf_op jit(solution)/shard_map/ppermute | solution.py:33
  106.8 7.3 %collective-permute-done.11 = bf16[3,128,896]{2,1,0:T(8,128)(2,1)S(1)} collective-permute-done((bf16[3,128,896]{2,1,0:T(8,128)(2,1)S(1)}, bf16[3,128,896]{2,1,0:T(8,128)(2,1)S(1)}, u32[]{:S(2)}, u32[]{:S(2)}) %collective-permute-start.11) | collective-permute-done | bytes 688160 | tf_op jit(solution)/shard_map/ppermute | solution.py:33
  127.1 6.9 %collective-permute-done.18 = bf16[3,32,896]{2,1,0:T(8,128)(2,1)S(1)} collective-permute-done((bf16[3,32,896]{2,1,0:T(8,128)(2,1)S(1)}, bf16[3,32,896]{2,1,0:T(8,128)(2,1)S(1)}, u32[]{:S(2)}, u32[]{:S(2)}) %collective-permute-start.18) | collective-permute-done | bytes 172064 | tf_op jit(solution)/shard_map/ppermute | solution.py:23
  134.0 4.1 %collective-permute-done.16 = bf16[3,32,896]{2,1,0:T(8,128)(2,1)S(1)} collective-permute-done((bf16[3,32,896]{2,1,0:T(8,128)(2,1)S(1)}, bf16[3,32,896]{2,1,0:T(8,128)(2,1)S(1)}, u32[]{:S(2)}, u32[]{:S(2)}) %collective-permute-start.16) | collective-permute-done | bytes 172064 | tf_op jit(solution)/shard_map/ppermute | solution.py:23
  138.2 3.7 %collective-permute-start.19 = (bf16[3,1,1]{2,1,0:T(2,128)(2,1)S(1)}, bf16[3,1,1]{2,1,0:T(2,128)(2,1)S(1)}, u32[]{:S(2)}, u32[]{:S(2)}) collective-permute-start(bf16[3,1,1]{2,1,0:T(2,128)(2,1)S(1)} %slice.146), channel_id=1, source_target_pairs={{0,1},{1,0},{2,3},{3,2},{4,5},{5,4},{6,7},{7,6},{8,9},{9,8},{10,11... | collective-permute-start | bytes 26 | tf_op jit(solution)/shard_map/ppermute | solution.py:37
  147.6 4.3 %collective-permute-done.21 = bf16[3,32,896]{2,1,0:T(8,128)(2,1)S(1)} collective-permute-done((bf16[3,32,896]{2,1,0:T(8,128)(2,1)S(1)}, bf16[3,32,896]{2,1,0:T(8,128)(2,1)S(1)}, u32[]{:S(2)}, u32[]{:S(2)}) %collective-permute-start.21) | collective-permute-done | bytes 172064 | tf_op jit(solution)/shard_map/ppermute | solution.py:33
  152.9 3.0 %collective-permute-start.26 = (bf16[2,128,896]{2,1,0:T(8,128)(2,1)S(1)}, bf16[2,128,896]{2,1,0:T(8,128)(2,1)S(1)}, u32[]{:S(2)}, u32[]{:S(2)}) collective-permute-start(bf16[2,128,896]{2,1,0:T(8,128)(2,1)S(1)} %slice.148), channel_id=1, source_target_pairs={{0,128},{1,33},{16,144},{17,49},{32,160},{33,1},{48,176},{49,17},{... | collective-permute-start | bytes 1376264 | tf_op jit(solution)/shard_map/ppermute | solution.py:33
  156.0 2.7 %collective-permute-start.28 = (bf16[2,128,896]{2,1,0:T(8,128)(2,1)S(1)}, bf16[2,128,896]{2,1,0:T(8,128)(2,1)S(1)}, u32[]{:S(2)}, u32[]{:S(2)}) collective-permute-start(bf16[2,128,896]{2,1,0:T(8,128)(2,1)S(1)} %slice.148), channel_id=1, source_target_pairs={{0,192},{1,49},{16,208},{17,1},{32,224},{33,17},{48,240},{49,33},{... | collective-permute-start | bytes 1376264 | tf_op jit(solution)/shard_map/ppermute | solution.py:33
  158.8 2.7 %collective-permute-start.25 = (bf16[1,128,896]{2,1,0:T(8,128)(2,1)S(1)}, bf16[1,128,896]{2,1,0:T(8,128)(2,1)S(1)}, u32[]{:S(2)}, u32[]{:S(2)}) collective-permute-start(bf16[1,128,896]{2,1,0:T(8,128)(2,1)S(1)} %slice.147), channel_id=1, source_target_pairs={{0,192},{1,49},{16,208},{17,1},{32,224},{33,17},{48,240},{49,33},{... | collective-permute-start | bytes 688136 | tf_op jit(solution)/shard_map/ppermute | solution.py:33
  161.5 9.6 %collective-permute-done.24 = bf16[1,128,896]{2,1,0:T(8,128)(2,1)S(1)} collective-permute-done((bf16[1,128,896]{2,1,0:T(8,128)(2,1)S(1)}, bf16[1,128,896]{2,1,0:T(8,128)(2,1)S(1)}, u32[]{:S(2)}, u32[]{:S(2)}) %collective-permute-start.24) | collective-permute-done | bytes 229408 | tf_op jit(solution)/shard_map/ppermute | solution.py:33
  175.3 2.5 %collective-permute-start.32 = (bf16[2,256,256]{2,1,0:T(8,128)(2,1)S(1)}, bf16[2,256,256]{2,1,0:T(8,128)(2,1)S(1)}, u32[]{:S(2)}, u32[]{:S(2)}) collective-permute-start(bf16[2,256,256]{2,1,0:T(8,128)(2,1)S(1)} %bitcast.203), channel_id=1, source_target_pairs={{0,1},{1,0},{2,3},{3,2},{4,5},{5,4},{6,7},{7,6},{8,9},{9,8},{10,11... | collective-permute-start | bytes 786440 | tf_op jit(solution)/shard_map/ppermute | solution.py:37
  180.6 2.5 %collective-permute-start.30 = (bf16[1,256,256]{2,1,0:T(8,128)(2,1)S(1)}, bf16[1,256,256]{2,1,0:T(8,128)(2,1)S(1)}, u32[]{:S(2)}, u32[]{:S(2)}) collective-permute-start(bf16[1,256,256]{2,1,0:T(8,128)(2,1)S(1)} %fusion.67), channel_id=1, source_target_pairs={{0,2},{2,0},{1,3},{3,1},{4,6},{6,4},{5,7},{7,5},{8,10},{10,8},{9,1... | collective-permute-start | bytes 393224 | tf_op jit(solution)/shard_map/ppermute | solution.py:37
  183.4 3.1 %collective-permute-done.30 = bf16[1,256,256]{2,1,0:T(8,128)(2,1)S(1)} collective-permute-done((bf16[1,256,256]{2,1,0:T(8,128)(2,1)S(1)}, bf16[1,256,256]{2,1,0:T(8,128)(2,1)S(1)}, u32[]{:S(2)}, u32[]{:S(2)}) %collective-permute-start.30) | collective-permute-done | bytes 131104 | tf_op jit(solution)/shard_map/ppermute | solution.py:37
  189.4 2.7 %collective-permute-done.33 = bf16[2,256,256]{2,1,0:T(8,128)(2,1)S(1)} collective-permute-done((bf16[2,256,256]{2,1,0:T(8,128)(2,1)S(1)}, bf16[2,256,256]{2,1,0:T(8,128)(2,1)S(1)}, u32[]{:S(2)}, u32[]{:S(2)}) %collective-permute-start.33) | collective-permute-done | bytes 262176 | tf_op jit(solution)/shard_map/ppermute | solution.py:37
  (144 shorter events, 60.3 us)
Async XLA Ops:
  24.3 7.6 %collective-permute-start.1 = (bf16[3,32,896]{2,1,0:T(8,128)(2,1)S(1)}, bf16[3,32,896]{2,1,0:T(8,128)(2,1)S(1)}, u32[]{:S(2)}, u32[]{:S(2)}) collective-permute-start(bf16[3,32,896]{2,1,0:T(8,128)(2,1)S(1)} %slice_bitcast_fusion.13), channel_id=1, source_target_pairs={{0,16},{1,65},{16,32},{17,81},{32,48},{33,97},{48,0},{49,113},{64,... | collective-permute-start | bytes 516104 | tf_op jit(solution)/shard_map/ppermute | solution.py:33
  24.3 7.6 %collective-permute-start = (bf16[3,32,896]{2,1,0:T(8,128)(2,1)S(1)}, bf16[3,32,896]{2,1,0:T(8,128)(2,1)S(1)}, u32[]{:S(2)}, u32[]{:S(2)}) collective-permute-start(bf16[3,32,896]{2,1,0:T(8,128)(2,1)S(1)} %slice_bitcast_fusion.13), channel_id=1, source_target_pairs={{0,32},{1,129},{16,48},{17,145},{32,0},{33,161},{48,16},{49,177},{... | collective-permute-start | bytes 516104 | tf_op jit(solution)/shard_map/ppermute | solution.py:33
  32.0 11.6 %collective-permute-start.3 = (bf16[3,128,896]{2,1,0:T(8,128)(2,1)S(1)}, bf16[3,128,896]{2,1,0:T(8,128)(2,1)}, u32[]{:S(2)}, u32[]{:S(2)}) collective-permute-start(bf16[3,128,896]{2,1,0:T(8,128)(2,1)S(1)} %pad_maximum_fusion.2), channel_id=1, source_target_pairs={{0,128},{1,33},{16,144},{17,49},{32,160},{33,1},{48,176},{49,17},{... | collective-permute-start | bytes 2064392 | tf_op jit(solution)/shard_map/ppermute | solution.py:33
  34.6 16.5 %collective-permute-start.4 = (bf16[3,128,896]{2,1,0:T(8,128)(2,1)S(1)}, bf16[3,128,896]{2,1,0:T(8,128)(2,1)}, u32[]{:S(2)}, u32[]{:S(2)}) collective-permute-start(bf16[3,128,896]{2,1,0:T(8,128)(2,1)S(1)} %pad_maximum_fusion.2), channel_id=1, source_target_pairs={{0,64},{1,17},{16,80},{17,33},{32,96},{33,49},{48,112},{49,1},{64,... | collective-permute-start | bytes 2064392 | tf_op jit(solution)/shard_map/ppermute | solution.py:33
  34.8 17.5 %collective-permute-start.5 = (bf16[3,128,896]{2,1,0:T(8,128)(2,1)S(1)}, bf16[3,128,896]{2,1,0:T(8,128)(2,1)S(1)}, u32[]{:S(2)}, u32[]{:S(2)}) collective-permute-start(bf16[3,128,896]{2,1,0:T(8,128)(2,1)S(1)} %pad_maximum_fusion.2), channel_id=1, source_target_pairs={{0,192},{1,49},{16,208},{17,1},{32,224},{33,17},{48,240},{49,33},{... | collective-permute-start | bytes 2064392 | tf_op jit(solution)/shard_map/ppermute | solution.py:33
  55.0 14.6 %collective-permute-start.6 = (f32[3,256,256]{2,1,0:T(8,128)}, f32[3,256,256]{2,1,0:T(8,128)S(1)}, u32[]{:S(2)}, u32[]{:S(2)}) collective-permute-start(f32[3,256,256]{2,1,0:T(8,128)} %bitcast.4), channel_id=1, source_target_pairs={{0,1},{1,0},{2,3},{3,2},{4,5},{5,4},{6,7},{7,6},{8,9},{9,8},{10,11... | collective-permute-start | bytes 2359304 | tf_op jit(solution)/shard_map/ppermute | solution.py:37
  70.5 10.5 %collective-permute-start.7 = (f32[3,128,256]{2,1,0:T(8,128)}, f32[3,128,256]{2,1,0:T(8,128)S(1)}, u32[]{:S(2)}, u32[]{:S(2)}) collective-permute-start(f32[3,128,256]{2,1,0:T(8,128)} %constant_dynamic-slice_fusion.3), channel_id=1, source_target_pairs={{0,2},{2,0},{1,3},{3,1},{4,6},{6,4},{5,7},{7,5},{8,10},{10,8},{9,1... | collective-permute-start | bytes 1179656 | tf_op jit(solution)/shard_map/ppermute | solution.py:37
  95.1 11.7 %collective-permute-start.12 = (bf16[3,128,896]{2,1,0:T(8,128)(2,1)S(1)}, bf16[3,128,896]{2,1,0:T(8,128)(2,1)S(1)}, u32[]{:S(2)}, u32[]{:S(2)}) collective-permute-start(bf16[3,128,896]{2,1,0:T(8,128)(2,1)S(1)} %get-tuple-element.5), channel_id=1, source_target_pairs={{0,128},{1,33},{16,144},{17,49},{32,160},{33,1},{48,176},{49,17},{... | collective-permute-start | bytes 2064392 | tf_op jit(solution)/shard_map/ppermute | solution.py:33
  95.2 18.9 %collective-permute-start.11 = (bf16[3,128,896]{2,1,0:T(8,128)(2,1)S(1)}, bf16[3,128,896]{2,1,0:T(8,128)(2,1)S(1)}, u32[]{:S(2)}, u32[]{:S(2)}) collective-permute-start(bf16[3,128,896]{2,1,0:T(8,128)(2,1)S(1)} %get-tuple-element.6), channel_id=1, source_target_pairs={{0,64},{1,17},{16,80},{17,33},{32,96},{33,49},{48,112},{49,1},{64,... | collective-permute-start | bytes 2064392 | tf_op jit(solution)/shard_map/ppermute | solution.py:33
  95.5 18.7 %collective-permute-start.10 = (bf16[3,128,896]{2,1,0:T(8,128)(2,1)S(1)}, bf16[3,128,896]{2,1,0:T(8,128)(2,1)S(1)}, u32[]{:S(2)}, u32[]{:S(2)}) collective-permute-start(bf16[3,128,896]{2,1,0:T(8,128)(2,1)S(1)} %get-tuple-element.4), channel_id=1, source_target_pairs={{0,192},{1,49},{16,208},{17,1},{32,224},{33,17},{48,240},{49,33},{... | collective-permute-start | bytes 2064392 | tf_op jit(solution)/shard_map/ppermute | solution.py:33
  114.6 6.1 %collective-permute-start.15 = (bf16[3,32,896]{2,1,0:T(8,128)(2,1)S(1)}, bf16[3,32,896]{2,1,0:T(8,128)(2,1)S(1)}, u32[]{:S(2)}, u32[]{:S(2)}) collective-permute-start(bf16[3,32,896]{2,1,0:T(8,128)(2,1)S(1)} %get-tuple-element.15), channel_id=1, source_target_pairs={{0,32},{1,129},{16,48},{17,145},{32,0},{33,161},{48,16},{49,177},{... | collective-permute-start | bytes 516104 | tf_op jit(solution)/shard_map/ppermute | solution.py:33
  122.7 11.2 %collective-permute-start.18 = (bf16[3,32,896]{2,1,0:T(8,128)(2,1)S(1)}, bf16[3,32,896]{2,1,0:T(8,128)(2,1)S(1)}, u32[]{:S(2)}, u32[]{:S(2)}) collective-permute-start(bf16[3,32,896]{2,1,0:T(8,128)(2,1)S(1)} %fusion.60), channel_id=1, source_target_pairs={{0,12},{4,0},{8,4},{12,8},{1,13},{5,1},{9,5},{13,9},{2,14},{6,2},{... | collective-permute-start | bytes 516104 | tf_op jit(solution)/shard_map/ppermute | solution.py:23
  123.3 10.6 %collective-permute-start.17 = (bf16[3,32,896]{2,1,0:T(8,128)(2,1)S(1)}, bf16[3,32,896]{2,1,0:T(8,128)(2,1)S(1)}, u32[]{:S(2)}, u32[]{:S(2)}) collective-permute-start(bf16[3,32,896]{2,1,0:T(8,128)(2,1)S(1)} %fusion.60), channel_id=1, source_target_pairs={{0,4},{4,8},{8,12},{12,0},{1,5},{5,9},{9,13},{13,1},{2,6},{6,10},{... | collective-permute-start | bytes 516104 | tf_op jit(solution)/shard_map/ppermute | solution.py:23
  125.2 12.9 %collective-permute-start.16 = (bf16[3,32,896]{2,1,0:T(8,128)(2,1)S(1)}, bf16[3,32,896]{2,1,0:T(8,128)(2,1)S(1)}, u32[]{:S(2)}, u32[]{:S(2)}) collective-permute-start(bf16[3,32,896]{2,1,0:T(8,128)(2,1)S(1)} %fusion.60), channel_id=1, source_target_pairs={{0,8},{4,12},{8,0},{12,4},{1,9},{5,13},{9,1},{13,5},{2,10},{6,14},... | collective-permute-start | bytes 516104 | tf_op jit(solution)/shard_map/ppermute | solution.py:23
  144.3 7.6 %collective-permute-start.21 = (bf16[3,32,896]{2,1,0:T(8,128)(2,1)S(1)}, bf16[3,32,896]{2,1,0:T(8,128)(2,1)S(1)}, u32[]{:S(2)}, u32[]{:S(2)}) collective-permute-start(bf16[3,32,896]{2,1,0:T(8,128)(2,1)S(1)} %broadcast_add_fusion), channel_id=1, source_target_pairs={{0,16},{1,65},{16,32},{17,81},{32,48},{33,97},{48,0},{49,113},{64,... | collective-permute-start | bytes 516104 | tf_op jit(solution)/shard_map/ppermute | solution.py:33
  144.6 7.3 %collective-permute-start.20 = (bf16[3,32,896]{2,1,0:T(8,128)(2,1)S(1)}, bf16[3,32,896]{2,1,0:T(8,128)(2,1)S(1)}, u32[]{:S(2)}, u32[]{:S(2)}) collective-permute-start(bf16[3,32,896]{2,1,0:T(8,128)(2,1)S(1)} %broadcast_add_fusion), channel_id=1, source_target_pairs={{0,32},{1,129},{16,48},{17,145},{32,0},{33,161},{48,16},{49,177},{... | collective-permute-start | bytes 516104 | tf_op jit(solution)/shard_map/ppermute | solution.py:33
  152.0 6.8 %collective-permute-start.23 = (bf16[1,128,896]{2,1,0:T(8,128)(2,1)S(1)}, bf16[1,128,896]{2,1,0:T(8,128)(2,1)S(1)}, u32[]{:S(2)}, u32[]{:S(2)}) collective-permute-start(bf16[1,128,896]{2,1,0:T(8,128)(2,1)S(1)} %slice.147), channel_id=1, source_target_pairs={{0,128},{1,33},{16,144},{17,49},{32,160},{33,1},{48,176},{49,17},{... | collective-permute-start | bytes 688136 | tf_op jit(solution)/shard_map/ppermute | solution.py:33
  152.9 18.7 %collective-permute-start.26 = (bf16[2,128,896]{2,1,0:T(8,128)(2,1)S(1)}, bf16[2,128,896]{2,1,0:T(8,128)(2,1)S(1)}, u32[]{:S(2)}, u32[]{:S(2)}) collective-permute-start(bf16[2,128,896]{2,1,0:T(8,128)(2,1)S(1)} %slice.148), channel_id=1, source_target_pairs={{0,128},{1,33},{16,144},{17,49},{32,160},{33,1},{48,176},{49,17},{... | collective-permute-start | bytes 1376264 | tf_op jit(solution)/shard_map/ppermute | solution.py:33
  155.9 15.7 %collective-permute-start.27 = (bf16[2,128,896]{2,1,0:T(8,128)(2,1)S(1)}, bf16[2,128,896]{2,1,0:T(8,128)(2,1)S(1)}, u32[]{:S(2)}, u32[]{:S(2)}) collective-permute-start(bf16[2,128,896]{2,1,0:T(8,128)(2,1)S(1)} %slice.148), channel_id=1, source_target_pairs={{0,64},{1,17},{16,80},{17,33},{32,96},{33,49},{48,112},{49,1},{64,... | collective-permute-start | bytes 1376264 | tf_op jit(solution)/shard_map/ppermute | solution.py:33
  156.0 15.8 %collective-permute-start.28 = (bf16[2,128,896]{2,1,0:T(8,128)(2,1)S(1)}, bf16[2,128,896]{2,1,0:T(8,128)(2,1)S(1)}, u32[]{:S(2)}, u32[]{:S(2)}) collective-permute-start(bf16[2,128,896]{2,1,0:T(8,128)(2,1)S(1)} %slice.148), channel_id=1, source_target_pairs={{0,192},{1,49},{16,208},{17,1},{32,224},{33,17},{48,240},{49,33},{... | collective-permute-start | bytes 1376264 | tf_op jit(solution)/shard_map/ppermute | solution.py:33
  158.6 12.4 %collective-permute-start.24 = (bf16[1,128,896]{2,1,0:T(8,128)(2,1)S(1)}, bf16[1,128,896]{2,1,0:T(8,128)(2,1)S(1)}, u32[]{:S(2)}, u32[]{:S(2)}) collective-permute-start(bf16[1,128,896]{2,1,0:T(8,128)(2,1)S(1)} %slice.147), channel_id=1, source_target_pairs={{0,64},{1,17},{16,80},{17,33},{32,96},{33,49},{48,112},{49,1},{64,... | collective-permute-start | bytes 688136 | tf_op jit(solution)/shard_map/ppermute | solution.py:33
  158.8 12.3 %collective-permute-start.25 = (bf16[1,128,896]{2,1,0:T(8,128)(2,1)S(1)}, bf16[1,128,896]{2,1,0:T(8,128)(2,1)S(1)}, u32[]{:S(2)}, u32[]{:S(2)}) collective-permute-start(bf16[1,128,896]{2,1,0:T(8,128)(2,1)S(1)} %slice.147), channel_id=1, source_target_pairs={{0,192},{1,49},{16,208},{17,1},{32,224},{33,17},{48,240},{49,33},{... | collective-permute-start | bytes 688136 | tf_op jit(solution)/shard_map/ppermute | solution.py:33
  175.3 7.8 %collective-permute-start.32 = (bf16[2,256,256]{2,1,0:T(8,128)(2,1)S(1)}, bf16[2,256,256]{2,1,0:T(8,128)(2,1)S(1)}, u32[]{:S(2)}, u32[]{:S(2)}) collective-permute-start(bf16[2,256,256]{2,1,0:T(8,128)(2,1)S(1)} %bitcast.203), channel_id=1, source_target_pairs={{0,1},{1,0},{2,3},{3,2},{4,5},{5,4},{6,7},{7,6},{8,9},{9,8},{10,11... | collective-permute-start | bytes 786440 | tf_op jit(solution)/shard_map/ppermute | solution.py:37
  183.3 8.8 %collective-permute-start.33 = (bf16[2,256,256]{2,1,0:T(8,128)(2,1)S(1)}, bf16[2,256,256]{2,1,0:T(8,128)(2,1)S(1)}, u32[]{:S(2)}, u32[]{:S(2)}) collective-permute-start(bf16[2,256,256]{2,1,0:T(8,128)(2,1)S(1)} %fusion.28), channel_id=1, source_target_pairs={{0,2},{2,0},{1,3},{3,1},{4,6},{6,4},{5,7},{7,5},{8,10},{10,8},{9,1... | collective-permute-start | bytes 786440 | tf_op jit(solution)/shard_map/ppermute | solution.py:37
  (19 other events, 147.8 us)
where the time goes:
time: 198 us
  waiting for transfers between devices  89.2 us (45%)
  starting transfers between devices  62.5 us (32%)
  blocking collectives  19.8 us (10%)
  matrix products  11.6 us (6%)
  local copies, waits for them, and re-layouts  9.39 us (5%)
  other arithmetic  3.9 us (2%)
    ppermute x21, waiting for transfers between devices, shift(): return lax.ppermute(value, ('y', 'x', 'core'), pairs)  52.4 us
    ppermute x21, starting transfers between devices, shift(): return lax.ppermute(value, ('y', 'x', 'core'), pairs)  29.9 us
    ppermute x11, starting transfers between devices, swap(): return lax.ppermute(value, axis, [(0, 1), (1, 0)])  28.3 us
    ppermute x11, waiting for transfers between devices, swap(): return lax.ppermute(value, axis, [(0, 1), (1, 0)])  25.9 us
    all_to_all x1, blocking collectives, gather_zh(): lax.all_to_all(copies, 'zh', split_axis=0, concat_axis=0, tiled=True)  19.8 us
    ppermute x3, waiting for transfers between devices, shift(): lax.ppermute(value, 'zh', [(i, (i + by) % RING) for i in range(RING)])  11 us
    ppermute x3, starting transfers between devices, shift(): lax.ppermute(value, 'zh', [(i, (i + by) % RING) for i in range(RING)])  4.34 us
  transfers between devices with their start and end apart: 35, of which 23 were waited for; matrix products, arithmetic and copies ran while one was open for 4% of the time, Pallas kernels for 0%

commit v1 on v0

--- a/solution.py
+++ b/solution.py
@@ -88,17 +88,14 @@
     return total
 
 
-def gather_zh(value):
-    copies = jnp.broadcast_to(value[None], (RING,) + value.shape)
-    got = lax.optimization_barrier(lax.all_to_all(copies, "zh", split_axis=0, concat_axis=0, tiled=True))
-    return jnp.moveaxis(got, 0, 1).reshape(value.shape[0], -1, value.shape[2])
-
-
 def fold_all(value):
-    total = value.astype(F32)
+    blocks = (value.shape[0], RING, -1, value.shape[2])
+    total = value.astype(F32).reshape(blocks)
     for s in ORDER[1:]:
-        total = total + shift(value, "zh", s).astype(F32)
-    return total
+        got = shift(value, "zh", s).reshape(blocks)
+        back = [ORDER.index((ORDER[i] - s) % RING) for i in range(RING)]
+        total = total + jnp.concatenate([got[:, i : i + 1] for i in back], axis=1).astype(F32)
+    return total.reshape(value.shape)
 
 
 def spread_wide(value):
@@ -113,7 +110,7 @@
 
 def on_device(acts_in, targets, enc_weight, enc_bias, dec_weight, dec_bias):
     layers = enc_weight.shape[0]
-    near = gather_zh(jnp.concatenate([acts_in, targets], axis=0))
+    near = lax.optimization_barrier(spread(jnp.concatenate([acts_in, targets], axis=0), "zh"))
     targets_near = near[layers:]
     acts = spread_wide(lax.optimization_barrier(spread(near[:layers], "first")))
     loss_scale = 1.0 / math.sqrt(acts.shape[1])
@@ -123,19 +120,18 @@
     half_feature = chip_join(jnp.maximum(pre_own, 0.0).astype(BF16))
     feature = core_join(half_feature)
 
-    totals = []
+    totals = jnp.zeros(acts.shape, BF16)
     for target in range(layers):
         total = 0.0
         for source in range(target + 1):
             total = total + jnp.dot(
                 feature[source], dec_weight[pair_index(source, target, layers)], preferred_element_type=F32
             )
-        totals.append(total.astype(BF16))
-    part = fold(lax.optimization_barrier(fold(jnp.stack(totals), "second")), "first")
+        totals = lax.dynamic_update_slice(totals, total.astype(BF16)[None], (target, 0, 0))
+    part = fold(lax.optimization_barrier(fold(totals, "second")), "first")
     recon = fold_all(part.astype(BF16))
     near = (recon + dec_bias[:, None, :] - targets_near.astype(F32)).astype(BF16)
-    rows = targets.shape[1]
-    errors = lax.dynamic_slice_in_dim(near, lax.axis_index("zh") * rows, rows, 1)
+    errors = near[:, : targets.shape[1]]
     near = near + swap(near[:, :1, :1], "core") * jnp.zeros((), BF16)
     err_first = lax.optimization_barrier(spread(near, "first"))
     late = spread_wide(err_first[1:])

time: 198 us -> 196 us (0.990)
  blocking collectives: 19.8 us -> 0 us
  starting transfers between devices: 62.5 us -> 73.7 us
  waiting for transfers between devices: 89.2 us -> 96.2 us
    all_to_all x1 -> x0, blocking collectives: 19.8 us -> none  [gather_zh(): lax.all_to_all(copies, 'zh', split_axis=0, concat_axis=0, tiled=True)]
    ppermute x3 -> x6, starting transfers between devices: 4.34 us -> 18 us  [shift(): lax.ppermute(value, 'zh', [(i, (i + by) % RING) for i in range(RING)])]
    ppermute x11, starting transfers between devices: 28.3 us -> 20.9 us  [swap(): return lax.ppermute(value, axis, [(0, 1), (1, 0)])]
    ppermute x21, starting transfers between devices: 29.9 us -> 34.8 us  [shift(): return lax.ppermute(value, ('y', 'x', 'core'), pairs)]
    ppermute x11, waiting for transfers between devices: 25.9 us -> 29.6 us  [swap(): return lax.ppermute(value, axis, [(0, 1), (1, 0)])]
    ppermute x3 -> x6, waiting for transfers between devices: 11 us -> 13.7 us  [shift(): lax.ppermute(value, 'zh', [(i, (i + by) % RING) for i in range(RING)])]
  transfers between devices with their start and end apart: 35 -> 38, of which waited for: 23 -> 29; matrix products, arithmetic and copies ran while one was open for 4% -> 4% of each run, Pallas kernels for 0% -> 0%
where the time goes in v1:
time: 196 us
  waiting for transfers between devices  96.2 us (49%)
  starting transfers between devices  73.7 us (38%)
  matrix products  11.7 us (6%)
  local copies, waits for them, and re-layouts  10.1 us (5%)
  other arithmetic  2.67 us (1%)
    ppermute x21, waiting for transfers between devices, shift(): return lax.ppermute(value, ('y', 'x', 'core'), pairs)  52.8 us
    ppermute x21, starting transfers between devices, shift(): return lax.ppermute(value, ('y', 'x', 'core'), pairs)  34.8 us
    ppermute x11, waiting for transfers between devices, swap(): return lax.ppermute(value, axis, [(0, 1), (1, 0)])  29.6 us
    ppermute x11, starting transfers between devices, swap(): return lax.ppermute(value, axis, [(0, 1), (1, 0)])  20.9 us
    ppermute x6, starting transfers between devices, shift(): lax.ppermute(value, 'zh', [(i, (i + by) % RING) for i in range(RING)])  18 us
    ppermute x6, waiting for transfers between devices, shift(): lax.ppermute(value, 'zh', [(i, (i + by) % RING) for i in range(RING)])  13.7 us
  transfers between devices with their start and end apart: 38, of which 29 were waited for; matrix products, arithmetic and copies ran while one was open for 4% of the time, Pallas kernels for 0%

profile of v1, /device:TPU:1, one launch (start us, length us, event | category | flops | bytes accessed | tf_op | source)
XLA Modules:
  0.0 195.6 jit_solution(17617127979038782409)
XLA Ops:
  2.3 7.7 %collective-permute-start = (bf16[6,8,896]{2,1,0:T(8,128)(2,1)S(1)}, bf16[6,8,896]{2,1,0:T(8,128)(2,1)S(1)}, u32[]{:S(2)}, u32[]{:S(2)}) collective-permute-start(bf16[6,8,896]{2,1,0:T(8,128)(2,1)S(1)} %constant_dynamic-update-slice_fusion), channel_id=1, source_target_pairs={{0,8},{4,12},{8,0},{12,4},{1,9},{5,13},{9,1},{13,5},{2,10},{6,14},... | collective-permute-start | bytes 258056 | tf_op jit(solution)/shard_map/ppermute | solution.py:23
  16.0 2.9 %collective-permute-done.2 = bf16[6,8,896]{2,1,0:T(8,128)(2,1)S(1)} collective-permute-done((bf16[6,8,896]{2,1,0:T(8,128)(2,1)S(1)}, bf16[6,8,896]{2,1,0:T(8,128)(2,1)S(1)}, u32[]{:S(2)}, u32[]{:S(2)}) %collective-permute-start.2) | collective-permute-done | bytes 86048 | tf_op jit(solution)/shard_map/ppermute | solution.py:23
  18.9 3.0 %collective-permute-start.3 = (bf16[3,32,896]{2,1,0:T(8,128)(2,1)S(1)}, bf16[3,32,896]{2,1,0:T(8,128)(2,1)S(1)}, u32[]{:S(2)}, u32[]{:S(2)}) collective-permute-start(bf16[3,32,896]{2,1,0:T(8,128)(2,1)S(1)} %slice.173), channel_id=1, source_target_pairs={{0,32},{1,129},{16,48},{17,145},{32,0},{33,161},{48,16},{49,177},{... | collective-permute-start | bytes 516104 | tf_op jit(solution)/shard_map/ppermute | solution.py:33
  25.1 2.6 %collective-permute-done.4 = bf16[3,32,896]{2,1,0:T(8,128)(2,1)S(1)} collective-permute-done((bf16[3,32,896]{2,1,0:T(8,128)(2,1)S(1)}, bf16[3,32,896]{2,1,0:T(8,128)(2,1)S(1)}, u32[]{:S(2)}, u32[]{:S(2)}) %collective-permute-start.4) | collective-permute-done | bytes 172064 | tf_op jit(solution)/shard_map/ppermute | solution.py:33
  27.8 2.5 %collective-permute-start.6 = (bf16[3,128,896]{2,1,0:T(8,128)(2,1)S(1)}, bf16[3,128,896]{2,1,0:T(8,128)(2,1)}, u32[]{:S(2)}, u32[]{:S(2)}) collective-permute-start(bf16[3,128,896]{2,1,0:T(8,128)(2,1)S(1)} %pad_maximum_fusion.1), channel_id=1, source_target_pairs={{0,128},{1,33},{16,144},{17,49},{32,160},{33,1},{48,176},{49,17},{... | collective-permute-start | bytes 2064392 | tf_op jit(solution)/shard_map/ppermute | solution.py:33
  33.2 6.4 %collective-permute-done.6 = bf16[3,128,896]{2,1,0:T(8,128)(2,1)} collective-permute-done((bf16[3,128,896]{2,1,0:T(8,128)(2,1)S(1)}, bf16[3,128,896]{2,1,0:T(8,128)(2,1)}, u32[]{:S(2)}, u32[]{:S(2)}) %collective-permute-start.6) | collective-permute-done | bytes 688160 | tf_op jit(solution)/shard_map/ppermute | solution.py:33
  40.8 6.1 %collective-permute-done.7 = bf16[3,128,896]{2,1,0:T(8,128)(2,1)} collective-permute-done((bf16[3,128,896]{2,1,0:T(8,128)(2,1)S(1)}, bf16[3,128,896]{2,1,0:T(8,128)(2,1)}, u32[]{:S(2)}, u32[]{:S(2)}) %collective-permute-start.7) | collective-permute-done | bytes 688160 | tf_op jit(solution)/shard_map/ppermute | solution.py:33
  50.7 2.6 %collective-permute-start.9 = (f32[3,256,256]{2,1,0:T(8,128)}, f32[3,256,256]{2,1,0:T(8,128)S(1)}, u32[]{:S(2)}, u32[]{:S(2)}) collective-permute-start(f32[3,256,256]{2,1,0:T(8,128)} %bitcast.2), channel_id=1, source_target_pairs={{0,1},{1,0},{2,3},{3,2},{4,5},{5,4},{6,7},{7,6},{8,9},{9,8},{10,11... | collective-permute-start | bytes 2359304 | tf_op jit(solution)/shard_map/ppermute | solution.py:37
  56.4 10.5 %collective-permute-done.10 = f32[3,128,256]{2,1,0:T(8,128)S(1)} collective-permute-done((f32[3,128,256]{2,1,0:T(8,128)}, f32[3,128,256]{2,1,0:T(8,128)S(1)}, u32[]{:S(2)}, u32[]{:S(2)}) %collective-permute-start.10) | collective-permute-done | bytes 393248 | tf_op jit(solution)/shard_map/ppermute | solution.py:37
  67.4 5.0 %collective-permute-done.11 = bf16[3,128,256]{2,1,0:T(8,128)(2,1)S(1)} collective-permute-done((bf16[3,128,256]{2,1,0:T(8,128)(2,1)S(1)}, bf16[3,128,256]{2,1,0:T(8,128)(2,1)S(1)}, u32[]{:S(2)}, u32[]{:S(2)}) %collective-permute-start.11) | collective-permute-done | bytes 196640 | tf_op jit(solution)/shard_map/ppermute | solution.py:37
  81.2 8.6 %collective-permute-start.13 = (bf16[3,128,896]{2,1,0:T(8,128)(2,1)S(1)}, bf16[3,128,896]{2,1,0:T(8,128)(2,1)S(1)}, u32[]{:S(2)}, u32[]{:S(2)}) collective-permute-start(bf16[3,128,896]{2,1,0:T(8,128)(2,1)S(1)} %get-tuple-element.4), channel_id=1, source_target_pairs={{0,192},{1,49},{16,208},{17,1},{32,224},{33,17},{48,240},{49,33},{... | collective-permute-start | bytes 2064392 | tf_op jit(solution)/shard_map/ppermute | solution.py:33
  91.1 14.0 %collective-permute-done.13 = bf16[3,128,896]{2,1,0:T(8,128)(2,1)S(1)} collective-permute-done((bf16[3,128,896]{2,1,0:T(8,128)(2,1)S(1)}, bf16[3,128,896]{2,1,0:T(8,128)(2,1)S(1)}, u32[]{:S(2)}, u32[]{:S(2)}) %collective-permute-start.13) | collective-permute-done | bytes 688160 | tf_op jit(solution)/shard_map/ppermute | solution.py:33
  105.1 3.1 %collective-permute-done.14 = bf16[3,128,896]{2,1,0:T(8,128)(2,1)S(1)} collective-permute-done((bf16[3,128,896]{2,1,0:T(8,128)(2,1)S(1)}, bf16[3,128,896]{2,1,0:T(8,128)(2,1)S(1)}, u32[]{:S(2)}, u32[]{:S(2)}) %collective-permute-start.14) | collective-permute-done | bytes 688160 | tf_op jit(solution)/shard_map/ppermute | solution.py:33
  114.5 2.7 %collective-permute-done.18 = bf16[3,32,896]{2,1,0:T(8,128)(2,1)S(1)} collective-permute-done((bf16[3,32,896]{2,1,0:T(8,128)(2,1)S(1)}, bf16[3,32,896]{2,1,0:T(8,128)(2,1)S(1)}, u32[]{:S(2)}, u32[]{:S(2)}) %collective-permute-start.18) | collective-permute-done | bytes 172064 | tf_op jit(solution)/shard_map/ppermute | solution.py:33
  117.3 4.5 %collective-permute-start.21 = (bf16[3,32,896]{2,1,0:T(8,128)(2,1)S(1)}, bf16[3,32,896]{2,1,0:T(8,128)(2,1)S(1)}, u32[]{:S(2)}, u32[]{:S(2)}) collective-permute-start(bf16[3,32,896]{2,1,0:T(8,128)(2,1)S(1)} %fusion.62), channel_id=1, source_target_pairs={{0,12},{4,0},{8,4},{12,8},{1,13},{5,1},{9,5},{13,9},{2,14},{6,2},{... | collective-permute-start | bytes 516104 | tf_op jit(solution)/shard_map/ppermute | solution.py:23
  124.7 7.4 %collective-permute-done.20 = bf16[3,32,896]{2,1,0:T(8,128)(2,1)S(1)} collective-permute-done((bf16[3,32,896]{2,1,0:T(8,128)(2,1)S(1)}, bf16[3,32,896]{2,1,0:T(8,128)(2,1)S(1)}, u32[]{:S(2)}, u32[]{:S(2)}) %collective-permute-start.20) | collective-permute-done | bytes 172064 | tf_op jit(solution)/shard_map/ppermute | solution.py:23
  132.8 5.5 %collective-permute-start.22 = (bf16[3,1,1]{2,1,0:T(2,128)(2,1)S(1)}, bf16[3,1,1]{2,1,0:T(2,128)(2,1)S(1)}, u32[]{:S(2)}, u32[]{:S(2)}) collective-permute-start(bf16[3,1,1]{2,1,0:T(2,128)(2,1)S(1)} %slice.200), channel_id=1, source_target_pairs={{0,1},{1,0},{2,3},{3,2},{4,5},{5,4},{6,7},{7,6},{8,9},{9,8},{10,11... | collective-permute-start | bytes 26 | tf_op jit(solution)/shard_map/ppermute | solution.py:37
  141.0 2.7 %collective-permute-start.25 = (bf16[3,32,896]{2,1,0:T(8,128)(2,1)S(1)}, bf16[3,32,896]{2,1,0:T(8,128)(2,1)S(1)}, u32[]{:S(2)}, u32[]{:S(2)}) collective-permute-start(bf16[3,32,896]{2,1,0:T(8,128)(2,1)S(1)} %broadcast_add_fusion), channel_id=1, source_target_pairs={{0,48},{1,193},{16,0},{17,209},{32,16},{33,225},{48,32},{49,241},{... | collective-permute-start | bytes 516104 | tf_op jit(solution)/shard_map/ppermute | solution.py:33
  148.3 2.6 %collective-permute-start.28 = (bf16[1,128,896]{2,1,0:T(8,128)(2,1)S(1)}, bf16[1,128,896]{2,1,0:T(8,128)(2,1)S(1)}, u32[]{:S(2)}, u32[]{:S(2)}) collective-permute-start(bf16[1,128,896]{2,1,0:T(8,128)(2,1)S(1)} %slice.201), channel_id=1, source_target_pairs={{0,192},{1,49},{16,208},{17,1},{32,224},{33,17},{48,240},{49,33},{... | collective-permute-start | bytes 688136 | tf_op jit(solution)/shard_map/ppermute | solution.py:33
  161.7 4.8 %collective-permute-done.30 = bf16[2,128,896]{2,1,0:T(8,128)(2,1)S(1)} collective-permute-done((bf16[2,128,896]{2,1,0:T(8,128)(2,1)S(1)}, bf16[2,128,896]{2,1,0:T(8,128)(2,1)S(1)}, u32[]{:S(2)}, u32[]{:S(2)}) %collective-permute-start.30) | collective-permute-done | bytes 458784 | tf_op jit(solution)/shard_map/ppermute | solution.py:33
  169.1 3.1 %collective-permute-start.32 = (bf16[1,256,256]{2,1,0:T(8,128)(2,1)S(1)}, bf16[1,256,256]{2,1,0:T(8,128)(2,1)S(1)}, u32[]{:S(2)}, u32[]{:S(2)}) collective-permute-start(bf16[1,256,256]{2,1,0:T(8,128)(2,1)S(1)} %bitcast.225), channel_id=1, source_target_pairs={{0,1},{1,0},{2,3},{3,2},{4,5},{5,4},{6,7},{7,6},{8,9},{9,8},{10,11... | collective-permute-start | bytes 393224 | tf_op jit(solution)/shard_map/ppermute | solution.py:37
  174.4 3.2 %collective-permute-start.33 = (bf16[1,256,256]{2,1,0:T(8,128)(2,1)S(1)}, bf16[1,256,256]{2,1,0:T(8,128)(2,1)S(1)}, u32[]{:S(2)}, u32[]{:S(2)}) collective-permute-start(bf16[1,256,256]{2,1,0:T(8,128)(2,1)S(1)} %fusion.71), channel_id=1, source_target_pairs={{0,2},{2,0},{1,3},{3,1},{4,6},{6,4},{5,7},{7,5},{8,10},{10,8},{9,1... | collective-permute-start | bytes 393224 | tf_op jit(solution)/shard_map/ppermute | solution.py:37
  178.1 2.9 %collective-permute-done.33 = bf16[1,256,256]{2,1,0:T(8,128)(2,1)S(1)} collective-permute-done((bf16[1,256,256]{2,1,0:T(8,128)(2,1)S(1)}, bf16[1,256,256]{2,1,0:T(8,128)(2,1)S(1)}, u32[]{:S(2)}, u32[]{:S(2)}) %collective-permute-start.33) | collective-permute-done | bytes 131104 | tf_op jit(solution)/shard_map/ppermute | solution.py:37
  184.5 5.8 %collective-permute-done.36 = bf16[2,256,256]{2,1,0:T(8,128)(2,1)S(1)} collective-permute-done((bf16[2,256,256]{2,1,0:T(8,128)(2,1)S(1)}, bf16[2,256,256]{2,1,0:T(8,128)(2,1)S(1)}, u32[]{:S(2)}, u32[]{:S(2)}) %collective-permute-start.36) | collective-permute-done | bytes 262176 | tf_op jit(solution)/shard_map/ppermute | solution.py:37
  (152 shorter events, 74.1 us)
Async XLA Ops:
  2.3 11.3 %collective-permute-start = (bf16[6,8,896]{2,1,0:T(8,128)(2,1)S(1)}, bf16[6,8,896]{2,1,0:T(8,128)(2,1)S(1)}, u32[]{:S(2)}, u32[]{:S(2)}) collective-permute-start(bf16[6,8,896]{2,1,0:T(8,128)(2,1)S(1)} %constant_dynamic-update-slice_fusion), channel_id=1, source_target_pairs={{0,8},{4,12},{8,0},{12,4},{1,9},{5,13},{9,1},{13,5},{2,10},{6,14},... | collective-permute-start | bytes 258056 | tf_op jit(solution)/shard_map/ppermute | solution.py:23
  11.3 7.6 %collective-permute-start.2 = (bf16[6,8,896]{2,1,0:T(8,128)(2,1)S(1)}, bf16[6,8,896]{2,1,0:T(8,128)(2,1)S(1)}, u32[]{:S(2)}, u32[]{:S(2)}) collective-permute-start(bf16[6,8,896]{2,1,0:T(8,128)(2,1)S(1)} %constant_dynamic-update-slice_fusion), channel_id=1, source_target_pairs={{0,12},{4,0},{8,4},{12,8},{1,13},{5,1},{9,5},{13,9},{2,14},{6,2},{... | collective-permute-start | bytes 258056 | tf_op jit(solution)/shard_map/ppermute | solution.py:23
  27.8 11.8 %collective-permute-start.6 = (bf16[3,128,896]{2,1,0:T(8,128)(2,1)S(1)}, bf16[3,128,896]{2,1,0:T(8,128)(2,1)}, u32[]{:S(2)}, u32[]{:S(2)}) collective-permute-start(bf16[3,128,896]{2,1,0:T(8,128)(2,1)S(1)} %pad_maximum_fusion.1), channel_id=1, source_target_pairs={{0,128},{1,33},{16,144},{17,49},{32,160},{33,1},{48,176},{49,17},{... | collective-permute-start | bytes 2064392 | tf_op jit(solution)/shard_map/ppermute | solution.py:33
  30.3 16.6 %collective-permute-start.7 = (bf16[3,128,896]{2,1,0:T(8,128)(2,1)S(1)}, bf16[3,128,896]{2,1,0:T(8,128)(2,1)}, u32[]{:S(2)}, u32[]{:S(2)}) collective-permute-start(bf16[3,128,896]{2,1,0:T(8,128)(2,1)S(1)} %pad_maximum_fusion.1), channel_id=1, source_target_pairs={{0,64},{1,17},{16,80},{17,33},{32,96},{33,49},{48,112},{49,1},{64,... | collective-permute-start | bytes 2064392 | tf_op jit(solution)/shard_map/ppermute | solution.py:33
  30.6 17.5 %collective-permute-start.8 = (bf16[3,128,896]{2,1,0:T(8,128)(2,1)S(1)}, bf16[3,128,896]{2,1,0:T(8,128)(2,1)S(1)}, u32[]{:S(2)}, u32[]{:S(2)}) collective-permute-start(bf16[3,128,896]{2,1,0:T(8,128)(2,1)S(1)} %pad_maximum_fusion.1), channel_id=1, source_target_pairs={{0,192},{1,49},{16,208},{17,1},{32,224},{33,17},{48,240},{49,33},{... | collective-permute-start | bytes 2064392 | tf_op jit(solution)/shard_map/ppermute | solution.py:33
  56.4 10.5 %collective-permute-start.10 = (f32[3,128,256]{2,1,0:T(8,128)}, f32[3,128,256]{2,1,0:T(8,128)S(1)}, u32[]{:S(2)}, u32[]{:S(2)}) collective-permute-start(f32[3,128,256]{2,1,0:T(8,128)} %constant_dynamic-slice_fusion.2), channel_id=1, source_target_pairs={{0,2},{2,0},{1,3},{3,1},{4,6},{6,4},{5,7},{7,5},{8,10},{10,8},{9,1... | collective-permute-start | bytes 1179656 | tf_op jit(solution)/shard_map/ppermute | solution.py:37
  81.2 23.8 %collective-permute-start.13 = (bf16[3,128,896]{2,1,0:T(8,128)(2,1)S(1)}, bf16[3,128,896]{2,1,0:T(8,128)(2,1)S(1)}, u32[]{:S(2)}, u32[]{:S(2)}) collective-permute-start(bf16[3,128,896]{2,1,0:T(8,128)(2,1)S(1)} %get-tuple-element.4), channel_id=1, source_target_pairs={{0,192},{1,49},{16,208},{17,1},{32,224},{33,17},{48,240},{49,33},{... | collective-permute-start | bytes 2064392 | tf_op jit(solution)/shard_map/ppermute | solution.py:33
  89.8 18.4 %collective-permute-start.14 = (bf16[3,128,896]{2,1,0:T(8,128)(2,1)S(1)}, bf16[3,128,896]{2,1,0:T(8,128)(2,1)S(1)}, u32[]{:S(2)}, u32[]{:S(2)}) collective-permute-start(bf16[3,128,896]{2,1,0:T(8,128)(2,1)S(1)} %get-tuple-element.6), channel_id=1, source_target_pairs={{0,64},{1,17},{16,80},{17,33},{32,96},{33,49},{48,112},{49,1},{64,... | collective-permute-start | bytes 2064392 | tf_op jit(solution)/shard_map/ppermute | solution.py:33
  89.8 18.4 %collective-permute-start.15 = (bf16[3,128,896]{2,1,0:T(8,128)(2,1)S(1)}, bf16[3,128,896]{2,1,0:T(8,128)(2,1)S(1)}, u32[]{:S(2)}, u32[]{:S(2)}) collective-permute-start(bf16[3,128,896]{2,1,0:T(8,128)(2,1)S(1)} %get-tuple-element.5), channel_id=1, source_target_pairs={{0,128},{1,33},{16,144},{17,49},{32,160},{33,1},{48,176},{49,17},{... | collective-permute-start | bytes 2064392 | tf_op jit(solution)/shard_map/ppermute | solution.py:33
  110.6 6.6 %collective-permute-start.18 = (bf16[3,32,896]{2,1,0:T(8,128)(2,1)S(1)}, bf16[3,32,896]{2,1,0:T(8,128)(2,1)S(1)}, u32[]{:S(2)}, u32[]{:S(2)}) collective-permute-start(bf16[3,32,896]{2,1,0:T(8,128)(2,1)S(1)} %get-tuple-element.15), channel_id=1, source_target_pairs={{0,32},{1,129},{16,48},{17,145},{32,0},{33,161},{48,16},{49,177},{... | collective-permute-start | bytes 516104 | tf_op jit(solution)/shard_map/ppermute | solution.py:33
  117.3 7.4 %collective-permute-start.21 = (bf16[3,32,896]{2,1,0:T(8,128)(2,1)S(1)}, bf16[3,32,896]{2,1,0:T(8,128)(2,1)S(1)}, u32[]{:S(2)}, u32[]{:S(2)}) collective-permute-start(bf16[3,32,896]{2,1,0:T(8,128)(2,1)S(1)} %fusion.62), channel_id=1, source_target_pairs={{0,12},{4,0},{8,4},{12,8},{1,13},{5,1},{9,5},{13,9},{2,14},{6,2},{... | collective-permute-start | bytes 516104 | tf_op jit(solution)/shard_map/ppermute | solution.py:23
  121.8 10.7 %collective-permute-start.19 = (bf16[3,32,896]{2,1,0:T(8,128)(2,1)S(1)}, bf16[3,32,896]{2,1,0:T(8,128)(2,1)S(1)}, u32[]{:S(2)}, u32[]{:S(2)}) collective-permute-start(bf16[3,32,896]{2,1,0:T(8,128)(2,1)S(1)} %fusion.62), channel_id=1, source_target_pairs={{0,8},{4,12},{8,0},{12,4},{1,9},{5,13},{9,1},{13,5},{2,10},{6,14},... | collective-permute-start | bytes 516104 | tf_op jit(solution)/shard_map/ppermute | solution.py:23
  121.9 10.3 %collective-permute-start.20 = (bf16[3,32,896]{2,1,0:T(8,128)(2,1)S(1)}, bf16[3,32,896]{2,1,0:T(8,128)(2,1)S(1)}, u32[]{:S(2)}, u32[]{:S(2)}) collective-permute-start(bf16[3,32,896]{2,1,0:T(8,128)(2,1)S(1)} %fusion.62), channel_id=1, source_target_pairs={{0,4},{4,8},{8,12},{12,0},{1,5},{5,9},{9,13},{13,1},{2,6},{6,10},{... | collective-permute-start | bytes 516104 | tf_op jit(solution)/shard_map/ppermute | solution.py:23
  132.8 6.3 %collective-permute-start.22 = (bf16[3,1,1]{2,1,0:T(2,128)(2,1)S(1)}, bf16[3,1,1]{2,1,0:T(2,128)(2,1)S(1)}, u32[]{:S(2)}, u32[]{:S(2)}) collective-permute-start(bf16[3,1,1]{2,1,0:T(2,128)(2,1)S(1)} %slice.200), channel_id=1, source_target_pairs={{0,1},{1,0},{2,3},{3,2},{4,5},{5,4},{6,7},{7,6},{8,9},{9,8},{10,11... | collective-permute-start | bytes 26 | tf_op jit(solution)/shard_map/ppermute | solution.py:37
  141.0 6.3 %collective-permute-start.24 = (bf16[3,32,896]{2,1,0:T(8,128)(2,1)S(1)}, bf16[3,32,896]{2,1,0:T(8,128)(2,1)S(1)}, u32[]{:S(2)}, u32[]{:S(2)}) collective-permute-start(bf16[3,32,896]{2,1,0:T(8,128)(2,1)S(1)} %broadcast_add_fusion), channel_id=1, source_target_pairs={{0,16},{1,65},{16,32},{17,81},{32,48},{33,97},{48,0},{49,113},{64,... | collective-permute-start | bytes 516104 | tf_op jit(solution)/shard_map/ppermute | solution.py:33
  147.4 6.8 %collective-permute-start.26 = (bf16[1,128,896]{2,1,0:T(8,128)(2,1)S(1)}, bf16[1,128,896]{2,1,0:T(8,128)(2,1)S(1)}, u32[]{:S(2)}, u32[]{:S(2)}) collective-permute-start(bf16[1,128,896]{2,1,0:T(8,128)(2,1)S(1)} %slice.201), channel_id=1, source_target_pairs={{0,128},{1,33},{16,144},{17,49},{32,160},{33,1},{48,176},{49,17},{... | collective-permute-start | bytes 688136 | tf_op jit(solution)/shard_map/ppermute | solution.py:33
  148.2 8.5 %collective-permute-start.27 = (bf16[1,128,896]{2,1,0:T(8,128)(2,1)S(1)}, bf16[1,128,896]{2,1,0:T(8,128)(2,1)S(1)}, u32[]{:S(2)}, u32[]{:S(2)}) collective-permute-start(bf16[1,128,896]{2,1,0:T(8,128)(2,1)S(1)} %slice.201), channel_id=1, source_target_pairs={{0,64},{1,17},{16,80},{17,33},{32,96},{33,49},{48,112},{49,1},{64,... | collective-permute-start | bytes 688136 | tf_op jit(solution)/shard_map/ppermute | solution.py:33
  148.3 10.4 %collective-permute-start.28 = (bf16[1,128,896]{2,1,0:T(8,128)(2,1)S(1)}, bf16[1,128,896]{2,1,0:T(8,128)(2,1)S(1)}, u32[]{:S(2)}, u32[]{:S(2)}) collective-permute-start(bf16[1,128,896]{2,1,0:T(8,128)(2,1)S(1)} %slice.201), channel_id=1, source_target_pairs={{0,192},{1,49},{16,208},{17,1},{32,224},{33,17},{48,240},{49,33},{... | collective-permute-start | bytes 688136 | tf_op jit(solution)/shard_map/ppermute | solution.py:33
  151.0 10.6 %collective-permute-start.29 = (bf16[2,128,896]{2,1,0:T(8,128)(2,1)S(1)}, bf16[2,128,896]{2,1,0:T(8,128)(2,1)S(1)}, u32[]{:S(2)}, u32[]{:S(2)}) collective-permute-start(bf16[2,128,896]{2,1,0:T(8,128)(2,1)S(1)} %slice.202), channel_id=1, source_target_pairs={{0,128},{1,33},{16,144},{17,49},{32,160},{33,1},{48,176},{49,17},{... | collective-permute-start | bytes 1376264 | tf_op jit(solution)/shard_map/ppermute | solution.py:33
  152.9 13.7 %collective-permute-start.30 = (bf16[2,128,896]{2,1,0:T(8,128)(2,1)S(1)}, bf16[2,128,896]{2,1,0:T(8,128)(2,1)S(1)}, u32[]{:S(2)}, u32[]{:S(2)}) collective-permute-start(bf16[2,128,896]{2,1,0:T(8,128)(2,1)S(1)} %slice.202), channel_id=1, source_target_pairs={{0,64},{1,17},{16,80},{17,33},{32,96},{33,49},{48,112},{49,1},{64,... | collective-permute-start | bytes 1376264 | tf_op jit(solution)/shard_map/ppermute | solution.py:33
  154.2 12.3 %collective-permute-start.31 = (bf16[2,128,896]{2,1,0:T(8,128)(2,1)S(1)}, bf16[2,128,896]{2,1,0:T(8,128)(2,1)S(1)}, u32[]{:S(2)}, u32[]{:S(2)}) collective-permute-start(bf16[2,128,896]{2,1,0:T(8,128)(2,1)S(1)} %slice.202), channel_id=1, source_target_pairs={{0,192},{1,49},{16,208},{17,1},{32,224},{33,17},{48,240},{49,33},{... | collective-permute-start | bytes 1376264 | tf_op jit(solution)/shard_map/ppermute | solution.py:33
  172.7 9.5 %collective-permute-start.35 = (bf16[2,256,256]{2,1,0:T(8,128)(2,1)S(1)}, bf16[2,256,256]{2,1,0:T(8,128)(2,1)S(1)}, u32[]{:S(2)}, u32[]{:S(2)}) collective-permute-start(bf16[2,256,256]{2,1,0:T(8,128)(2,1)S(1)} %bitcast.213), channel_id=1, source_target_pairs={{0,1},{1,0},{2,3},{3,2},{4,5},{5,4},{6,7},{7,6},{8,9},{9,8},{10,11... | collective-permute-start | bytes 786440 | tf_op jit(solution)/shard_map/ppermute | solution.py:37
  174.4 6.5 %collective-permute-start.33 = (bf16[1,256,256]{2,1,0:T(8,128)(2,1)S(1)}, bf16[1,256,256]{2,1,0:T(8,128)(2,1)S(1)}, u32[]{:S(2)}, u32[]{:S(2)}) collective-permute-start(bf16[1,256,256]{2,1,0:T(8,128)(2,1)S(1)} %fusion.71), channel_id=1, source_target_pairs={{0,2},{2,0},{1,3},{3,1},{4,6},{6,4},{5,7},{7,5},{8,10},{10,8},{9,1... | collective-permute-start | bytes 393224 | tf_op jit(solution)/shard_map/ppermute | solution.py:37
  182.4 7.9 %collective-permute-start.36 = (bf16[2,256,256]{2,1,0:T(8,128)(2,1)S(1)}, bf16[2,256,256]{2,1,0:T(8,128)(2,1)S(1)}, u32[]{:S(2)}, u32[]{:S(2)}) collective-permute-start(bf16[2,256,256]{2,1,0:T(8,128)(2,1)S(1)} %fusion.30), channel_id=1, source_target_pairs={{0,2},{2,0},{1,3},{3,1},{4,6},{6,4},{5,7},{7,5},{8,10},{10,8},{9,1... | collective-permute-start | bytes 786440 | tf_op jit(solution)/shard_map/ppermute | solution.py:37
  (21 other events, 166.9 us)

commit v2 on v1

--- a/solution.py
+++ b/solution.py
@@ -74,6 +74,10 @@
     return jnp.concatenate([jnp.where(first, value, got), jnp.where(first, got, value)], axis=1)
 
 
+def in_step(value):
+    return value + swap(value[:1, :1, :1], "core") * jnp.zeros((), value.dtype)
+
+
 def spread(value, stage):
     slots = {s: shift(value, stage, s) for s in ORDER[1:]}
     return jnp.concatenate([value] + [slots[s] for s in ORDER[1:]], axis=1)
@@ -128,11 +132,11 @@
                 feature[source], dec_weight[pair_index(source, target, layers)], preferred_element_type=F32
             )
         totals = lax.dynamic_update_slice(totals, total.astype(BF16)[None], (target, 0, 0))
-    part = fold(lax.optimization_barrier(fold(totals, "second")), "first")
+    wide = in_step(fold(totals, "second").astype(BF16))
+    part = fold(lax.optimization_barrier(wide), "first")
     recon = fold_all(part.astype(BF16))
     near = (recon + dec_bias[:, None, :] - targets_near.astype(F32)).astype(BF16)
     errors = near[:, : targets.shape[1]]
-    near = near + swap(near[:, :1, :1], "core") * jnp.zeros((), BF16)
     err_first = lax.optimization_barrier(spread(near, "first"))
     late = spread_wide(err_first[1:])
     early = spread_wide(err_first[:1])

time: 196 us -> 198 us (1.010)
  transfers between devices with their start and end apart: 38 -> 38, of which waited for: 29 -> 27; matrix products, arithmetic and copies ran while one was open for 4% -> 4% of each run, Pallas kernels for 0% -> 0%
where the time goes in v2:
time: 198 us; the launch traced here: 197 us
  waiting for transfers between devices  96.4 us (49%)
  starting transfers between devices  73.8 us (37%)
  matrix products  11.7 us (6%)
  local copies, waits for them, and re-layouts  10.7 us (5%)
  other arithmetic  2.49 us (1%)
    ppermute x21, waiting for transfers between devices, shift(): return lax.ppermute(value, ('y', 'x', 'core'), pairs)  52.5 us
    ppermute x21, starting transfers between devices, shift(): return lax.ppermute(value, ('y', 'x', 'core'), pairs)  36.5 us
    ppermute x11, waiting for transfers between devices, swap(): return lax.ppermute(value, axis, [(0, 1), (1, 0)])  30.1 us
    ppermute x11, starting transfers between devices, swap(): return lax.ppermute(value, axis, [(0, 1), (1, 0)])  19.3 us
    ppermute x6, starting transfers between devices, shift(): lax.ppermute(value, 'zh', [(i, (i + by) % RING) for i in range(RING)])  18 us
    ppermute x6, waiting for transfers between devices, shift(): lax.ppermute(value, 'zh', [(i, (i + by) % RING) for i in range(RING)])  13.7 us
  transfers between devices with their start and end apart: 38, of which 27 were waited for; matrix products, arithmetic and copies ran while one was open for 4% of the time, Pallas kernels for 0%

profile of v2, /device:TPU:1, one launch (start us, length us, event | category | flops | bytes accessed | tf_op | source)
XLA Modules:
  0.0 196.8 jit_solution(6720056010586548364)
XLA Ops:
  2.3 7.7 %collective-permute-start = (bf16[6,8,896]{2,1,0:T(8,128)(2,1)S(1)}, bf16[6,8,896]{2,1,0:T(8,128)(2,1)S(1)}, u32[]{:S(2)}, u32[]{:S(2)}) collective-permute-start(bf16[6,8,896]{2,1,0:T(8,128)(2,1)S(1)} %constant_dynamic-update-slice_fusion), channel_id=1, source_target_pairs={{0,8},{4,12},{8,0},{12,4},{1,9},{5,13},{9,1},{13,5},{2,10},{6,14},... | collective-permute-start | bytes 258056 | tf_op jit(solution)/shard_map/ppermute | solution.py:23
  11.3 2.4 %collective-permute-start.2 = (bf16[6,8,896]{2,1,0:T(8,128)(2,1)S(1)}, bf16[6,8,896]{2,1,0:T(8,128)(2,1)S(1)}, u32[]{:S(2)}, u32[]{:S(2)}) collective-permute-start(bf16[6,8,896]{2,1,0:T(8,128)(2,1)S(1)} %constant_dynamic-update-slice_fusion), channel_id=1, source_target_pairs={{0,12},{4,0},{8,4},{12,8},{1,13},{5,1},{9,5},{13,9},{2,14},{6,2},{... | collective-permute-start | bytes 258056 | tf_op jit(solution)/shard_map/ppermute | solution.py:23
  16.0 2.9 %collective-permute-done.2 = bf16[6,8,896]{2,1,0:T(8,128)(2,1)S(1)} collective-permute-done((bf16[6,8,896]{2,1,0:T(8,128)(2,1)S(1)}, bf16[6,8,896]{2,1,0:T(8,128)(2,1)S(1)}, u32[]{:S(2)}, u32[]{:S(2)}) %collective-permute-start.2) | collective-permute-done | bytes 86048 | tf_op jit(solution)/shard_map/ppermute | solution.py:23
  18.9 3.0 %collective-permute-start.3 = (bf16[3,32,896]{2,1,0:T(8,128)(2,1)S(1)}, bf16[3,32,896]{2,1,0:T(8,128)(2,1)S(1)}, u32[]{:S(2)}, u32[]{:S(2)}) collective-permute-start(bf16[3,32,896]{2,1,0:T(8,128)(2,1)S(1)} %slice.170), channel_id=1, source_target_pairs={{0,32},{1,129},{16,48},{17,145},{32,0},{33,161},{48,16},{49,177},{... | collective-permute-start | bytes 516104 | tf_op jit(solution)/shard_map/ppermute | solution.py:33
  25.1 2.6 %collective-permute-done.4 = bf16[3,32,896]{2,1,0:T(8,128)(2,1)S(1)} collective-permute-done((bf16[3,32,896]{2,1,0:T(8,128)(2,1)S(1)}, bf16[3,32,896]{2,1,0:T(8,128)(2,1)S(1)}, u32[]{:S(2)}, u32[]{:S(2)}) %collective-permute-start.4) | collective-permute-done | bytes 172064 | tf_op jit(solution)/shard_map/ppermute | solution.py:33
  27.8 2.5 %collective-permute-start.6 = (bf16[3,128,896]{2,1,0:T(8,128)(2,1)S(1)}, bf16[3,128,896]{2,1,0:T(8,128)(2,1)}, u32[]{:S(2)}, u32[]{:S(2)}) collective-permute-start(bf16[3,128,896]{2,1,0:T(8,128)(2,1)S(1)} %pad_maximum_fusion.1), channel_id=1, source_target_pairs={{0,128},{1,33},{16,144},{17,49},{32,160},{33,1},{48,176},{49,17},{... | collective-permute-start | bytes 2064392 | tf_op jit(solution)/shard_map/ppermute | solution.py:33
  33.2 6.4 %collective-permute-done.6 = bf16[3,128,896]{2,1,0:T(8,128)(2,1)} collective-permute-done((bf16[3,128,896]{2,1,0:T(8,128)(2,1)S(1)}, bf16[3,128,896]{2,1,0:T(8,128)(2,1)}, u32[]{:S(2)}, u32[]{:S(2)}) %collective-permute-start.6) | collective-permute-done | bytes 688160 | tf_op jit(solution)/shard_map/ppermute | solution.py:33
  40.8 6.1 %collective-permute-done.7 = bf16[3,128,896]{2,1,0:T(8,128)(2,1)} collective-permute-done((bf16[3,128,896]{2,1,0:T(8,128)(2,1)S(1)}, bf16[3,128,896]{2,1,0:T(8,128)(2,1)}, u32[]{:S(2)}, u32[]{:S(2)}) %collective-permute-start.7) | collective-permute-done | bytes 688160 | tf_op jit(solution)/shard_map/ppermute | solution.py:33
  50.7 2.6 %collective-permute-start.9 = (f32[3,256,256]{2,1,0:T(8,128)}, f32[3,256,256]{2,1,0:T(8,128)S(1)}, u32[]{:S(2)}, u32[]{:S(2)}) collective-permute-start(f32[3,256,256]{2,1,0:T(8,128)} %bitcast.2), channel_id=1, source_target_pairs={{0,1},{1,0},{2,3},{3,2},{4,5},{5,4},{6,7},{7,6},{8,9},{9,8},{10,11... | collective-permute-start | bytes 2359304 | tf_op jit(solution)/shard_map/ppermute | solution.py:37
  56.5 10.5 %collective-permute-done.10 = f32[3,128,256]{2,1,0:T(8,128)S(1)} collective-permute-done((f32[3,128,256]{2,1,0:T(8,128)}, f32[3,128,256]{2,1,0:T(8,128)S(1)}, u32[]{:S(2)}, u32[]{:S(2)}) %collective-permute-start.10) | collective-permute-done | bytes 393248 | tf_op jit(solution)/shard_map/ppermute | solution.py:37
  67.4 5.0 %collective-permute-done.11 = bf16[3,128,256]{2,1,0:T(8,128)(2,1)S(1)} collective-permute-done((bf16[3,128,256]{2,1,0:T(8,128)(2,1)S(1)}, bf16[3,128,256]{2,1,0:T(8,128)(2,1)S(1)}, u32[]{:S(2)}, u32[]{:S(2)}) %collective-permute-start.11) | collective-permute-done | bytes 196640 | tf_op jit(solution)/shard_map/ppermute | solution.py:37
  81.2 8.6 %collective-permute-start.13 = (bf16[3,128,896]{2,1,0:T(8,128)(2,1)S(1)}, bf16[3,128,896]{2,1,0:T(8,128)(2,1)S(1)}, u32[]{:S(2)}, u32[]{:S(2)}) collective-permute-start(bf16[3,128,896]{2,1,0:T(8,128)(2,1)S(1)} %get-tuple-element.4), channel_id=1, source_target_pairs={{0,192},{1,49},{16,208},{17,1},{32,224},{33,17},{48,240},{49,33},{... | collective-permute-start | bytes 2064392 | tf_op jit(solution)/shard_map/ppermute | solution.py:33
  91.1 14.0 %collective-permute-done.13 = bf16[3,128,896]{2,1,0:T(8,128)(2,1)S(1)} collective-permute-done((bf16[3,128,896]{2,1,0:T(8,128)(2,1)S(1)}, bf16[3,128,896]{2,1,0:T(8,128)(2,1)S(1)}, u32[]{:S(2)}, u32[]{:S(2)}) %collective-permute-start.13) | collective-permute-done | bytes 688160 | tf_op jit(solution)/shard_map/ppermute | solution.py:33
  105.1 3.1 %collective-permute-done.14 = bf16[3,128,896]{2,1,0:T(8,128)(2,1)S(1)} collective-permute-done((bf16[3,128,896]{2,1,0:T(8,128)(2,1)S(1)}, bf16[3,128,896]{2,1,0:T(8,128)(2,1)S(1)}, u32[]{:S(2)}, u32[]{:S(2)}) %collective-permute-start.14) | collective-permute-done | bytes 688160 | tf_op jit(solution)/shard_map/ppermute | solution.py:33
  117.1 2.7 %collective-permute-done.19 = bf16[3,32,896]{2,1,0:T(8,128)(2,1)S(1)} collective-permute-done((bf16[3,32,896]{2,1,0:T(8,128)(2,1)S(1)}, bf16[3,32,896]{2,1,0:T(8,128)(2,1)S(1)}, u32[]{:S(2)}, u32[]{:S(2)}) %collective-permute-start.19) | collective-permute-done | bytes 172064 | tf_op jit(solution)/shard_map/ppermute | solution.py:33
  119.9 4.5 %collective-permute-start.22 = (bf16[3,32,896]{2,1,0:T(8,128)(2,1)S(1)}, bf16[3,32,896]{2,1,0:T(8,128)(2,1)S(1)}, u32[]{:S(2)}, u32[]{:S(2)}) collective-permute-start(bf16[3,32,896]{2,1,0:T(8,128)(2,1)S(1)} %add_convert_fusion.3), channel_id=1, source_target_pairs={{0,12},{4,0},{8,4},{12,8},{1,13},{5,1},{9,5},{13,9},{2,14},{6,2},{... | collective-permute-start | bytes 516104 | tf_op jit(solution)/shard_map/ppermute | solution.py:23
  127.3 7.4 %collective-permute-done.21 = bf16[3,32,896]{2,1,0:T(8,128)(2,1)S(1)} collective-permute-done((bf16[3,32,896]{2,1,0:T(8,128)(2,1)S(1)}, bf16[3,32,896]{2,1,0:T(8,128)(2,1)S(1)}, u32[]{:S(2)}, u32[]{:S(2)}) %collective-permute-start.21) | collective-permute-done | bytes 172064 | tf_op jit(solution)/shard_map/ppermute | solution.py:23
  135.3 2.8 %collective-permute-start.23 = (bf16[3,32,896]{2,1,0:T(8,128)(2,1)S(1)}, bf16[3,32,896]{2,1,0:T(8,128)(2,1)S(1)}, u32[]{:S(2)}, u32[]{:S(2)}) collective-permute-start(bf16[3,32,896]{2,1,0:T(8,128)(2,1)S(1)} %fusion.62), channel_id=1, source_target_pairs={{0,32},{1,129},{16,48},{17,145},{32,0},{33,161},{48,16},{49,177},{... | collective-permute-start | bytes 516104 | tf_op jit(solution)/shard_map/ppermute | solution.py:33
  141.6 2.8 %collective-permute-done.24 = bf16[3,32,896]{2,1,0:T(8,128)(2,1)S(1)} collective-permute-done((bf16[3,32,896]{2,1,0:T(8,128)(2,1)S(1)}, bf16[3,32,896]{2,1,0:T(8,128)(2,1)S(1)}, u32[]{:S(2)}, u32[]{:S(2)}) %collective-permute-start.24) | collective-permute-done | bytes 172064 | tf_op jit(solution)/shard_map/ppermute | solution.py:33
  154.4 4.8 %collective-permute-done.29 = bf16[2,128,896]{2,1,0:T(8,128)(2,1)S(1)} collective-permute-done((bf16[2,128,896]{2,1,0:T(8,128)(2,1)S(1)}, bf16[2,128,896]{2,1,0:T(8,128)(2,1)S(1)}, u32[]{:S(2)}, u32[]{:S(2)}) %collective-permute-start.29) | collective-permute-done | bytes 458784 | tf_op jit(solution)/shard_map/ppermute | solution.py:33
  159.2 4.7 %collective-permute-done.30 = bf16[2,128,896]{2,1,0:T(8,128)(2,1)S(1)} collective-permute-done((bf16[2,128,896]{2,1,0:T(8,128)(2,1)S(1)}, bf16[2,128,896]{2,1,0:T(8,128)(2,1)S(1)}, u32[]{:S(2)}, u32[]{:S(2)}) %collective-permute-start.30) | collective-permute-done | bytes 458784 | tf_op jit(solution)/shard_map/ppermute | solution.py:33
  166.5 8.5 %collective-permute-start.32 = (bf16[1,256,256]{2,1,0:T(8,128)(2,1)S(1)}, bf16[1,256,256]{2,1,0:T(8,128)(2,1)S(1)}, u32[]{:S(2)}, u32[]{:S(2)}) collective-permute-start(bf16[1,256,256]{2,1,0:T(8,128)(2,1)S(1)} %bitcast.226), channel_id=1, source_target_pairs={{0,1},{1,0},{2,3},{3,2},{4,5},{5,4},{6,7},{7,6},{8,9},{9,8},{10,11... | collective-permute-start | bytes 393224 | tf_op jit(solution)/shard_map/ppermute | solution.py:37
  179.2 2.7 %collective-permute-done.33 = bf16[1,256,256]{2,1,0:T(8,128)(2,1)S(1)} collective-permute-done((bf16[1,256,256]{2,1,0:T(8,128)(2,1)S(1)}, bf16[1,256,256]{2,1,0:T(8,128)(2,1)S(1)}, u32[]{:S(2)}, u32[]{:S(2)}) %collective-permute-start.33) | collective-permute-done | bytes 131104 | tf_op jit(solution)/shard_map/ppermute | solution.py:37
  185.6 6.0 %collective-permute-done.36 = bf16[2,256,256]{2,1,0:T(8,128)(2,1)S(1)} collective-permute-done((bf16[2,256,256]{2,1,0:T(8,128)(2,1)S(1)}, bf16[2,256,256]{2,1,0:T(8,128)(2,1)S(1)}, u32[]{:S(2)}, u32[]{:S(2)}) %collective-permute-start.36) | collective-permute-done | bytes 262176 | tf_op jit(solution)/shard_map/ppermute | solution.py:37
  (150 shorter events, 70.6 us)
Async XLA Ops:
  2.3 11.3 %collective-permute-start = (bf16[6,8,896]{2,1,0:T(8,128)(2,1)S(1)}, bf16[6,8,896]{2,1,0:T(8,128)(2,1)S(1)}, u32[]{:S(2)}, u32[]{:S(2)}) collective-permute-start(bf16[6,8,896]{2,1,0:T(8,128)(2,1)S(1)} %constant_dynamic-update-slice_fusion), channel_id=1, source_target_pairs={{0,8},{4,12},{8,0},{12,4},{1,9},{5,13},{9,1},{13,5},{2,10},{6,14},... | collective-permute-start | bytes 258056 | tf_op jit(solution)/shard_map/ppermute | solution.py:23
  11.3 7.6 %collective-permute-start.2 = (bf16[6,8,896]{2,1,0:T(8,128)(2,1)S(1)}, bf16[6,8,896]{2,1,0:T(8,128)(2,1)S(1)}, u32[]{:S(2)}, u32[]{:S(2)}) collective-permute-start(bf16[6,8,896]{2,1,0:T(8,128)(2,1)S(1)} %constant_dynamic-update-slice_fusion), channel_id=1, source_target_pairs={{0,12},{4,0},{8,4},{12,8},{1,13},{5,1},{9,5},{13,9},{2,14},{6,2},{... | collective-permute-start | bytes 258056 | tf_op jit(solution)/shard_map/ppermute | solution.py:23
  27.8 11.8 %collective-permute-start.6 = (bf16[3,128,896]{2,1,0:T(8,128)(2,1)S(1)}, bf16[3,128,896]{2,1,0:T(8,128)(2,1)}, u32[]{:S(2)}, u32[]{:S(2)}) collective-permute-start(bf16[3,128,896]{2,1,0:T(8,128)(2,1)S(1)} %pad_maximum_fusion.1), channel_id=1, source_target_pairs={{0,128},{1,33},{16,144},{17,49},{32,160},{33,1},{48,176},{49,17},{... | collective-permute-start | bytes 2064392 | tf_op jit(solution)/shard_map/ppermute | solution.py:33
  30.3 16.6 %collective-permute-start.7 = (bf16[3,128,896]{2,1,0:T(8,128)(2,1)S(1)}, bf16[3,128,896]{2,1,0:T(8,128)(2,1)}, u32[]{:S(2)}, u32[]{:S(2)}) collective-permute-start(bf16[3,128,896]{2,1,0:T(8,128)(2,1)S(1)} %pad_maximum_fusion.1), channel_id=1, source_target_pairs={{0,64},{1,17},{16,80},{17,33},{32,96},{33,49},{48,112},{49,1},{64,... | collective-permute-start | bytes 2064392 | tf_op jit(solution)/shard_map/ppermute | solution.py:33
  30.6 17.5 %collective-permute-start.8 = (bf16[3,128,896]{2,1,0:T(8,128)(2,1)S(1)}, bf16[3,128,896]{2,1,0:T(8,128)(2,1)S(1)}, u32[]{:S(2)}, u32[]{:S(2)}) collective-permute-start(bf16[3,128,896]{2,1,0:T(8,128)(2,1)S(1)} %pad_maximum_fusion.1), channel_id=1, source_target_pairs={{0,192},{1,49},{16,208},{17,1},{32,224},{33,17},{48,240},{49,33},{... | collective-permute-start | bytes 2064392 | tf_op jit(solution)/shard_map/ppermute | solution.py:33
  56.4 10.5 %collective-permute-start.10 = (f32[3,128,256]{2,1,0:T(8,128)}, f32[3,128,256]{2,1,0:T(8,128)S(1)}, u32[]{:S(2)}, u32[]{:S(2)}) collective-permute-start(f32[3,128,256]{2,1,0:T(8,128)} %constant_dynamic-slice_fusion.2), channel_id=1, source_target_pairs={{0,2},{2,0},{1,3},{3,1},{4,6},{6,4},{5,7},{7,5},{8,10},{10,8},{9,1... | collective-permute-start | bytes 1179656 | tf_op jit(solution)/shard_map/ppermute | solution.py:37
  81.2 23.8 %collective-permute-start.13 = (bf16[3,128,896]{2,1,0:T(8,128)(2,1)S(1)}, bf16[3,128,896]{2,1,0:T(8,128)(2,1)S(1)}, u32[]{:S(2)}, u32[]{:S(2)}) collective-permute-start(bf16[3,128,896]{2,1,0:T(8,128)(2,1)S(1)} %get-tuple-element.4), channel_id=1, source_target_pairs={{0,192},{1,49},{16,208},{17,1},{32,224},{33,17},{48,240},{49,33},{... | collective-permute-start | bytes 2064392 | tf_op jit(solution)/shard_map/ppermute | solution.py:33
  89.8 18.4 %collective-permute-start.14 = (bf16[3,128,896]{2,1,0:T(8,128)(2,1)S(1)}, bf16[3,128,896]{2,1,0:T(8,128)(2,1)S(1)}, u32[]{:S(2)}, u32[]{:S(2)}) collective-permute-start(bf16[3,128,896]{2,1,0:T(8,128)(2,1)S(1)} %get-tuple-element.6), channel_id=1, source_target_pairs={{0,64},{1,17},{16,80},{17,33},{32,96},{33,49},{48,112},{49,1},{64,... | collective-permute-start | bytes 2064392 | tf_op jit(solution)/shard_map/ppermute | solution.py:33
  89.8 18.4 %collective-permute-start.15 = (bf16[3,128,896]{2,1,0:T(8,128)(2,1)S(1)}, bf16[3,128,896]{2,1,0:T(8,128)(2,1)S(1)}, u32[]{:S(2)}, u32[]{:S(2)}) collective-permute-start(bf16[3,128,896]{2,1,0:T(8,128)(2,1)S(1)} %get-tuple-element.5), channel_id=1, source_target_pairs={{0,128},{1,33},{16,144},{17,49},{32,160},{33,1},{48,176},{49,17},{... | collective-permute-start | bytes 2064392 | tf_op jit(solution)/shard_map/ppermute | solution.py:33
  113.2 6.6 %collective-permute-start.19 = (bf16[3,32,896]{2,1,0:T(8,128)(2,1)S(1)}, bf16[3,32,896]{2,1,0:T(8,128)(2,1)S(1)}, u32[]{:S(2)}, u32[]{:S(2)}) collective-permute-start(bf16[3,32,896]{2,1,0:T(8,128)(2,1)S(1)} %get-tuple-element.15), channel_id=1, source_target_pairs={{0,32},{1,129},{16,48},{17,145},{32,0},{33,161},{48,16},{49,177},{... | collective-permute-start | bytes 516104 | tf_op jit(solution)/shard_map/ppermute | solution.py:33
  119.9 7.3 %collective-permute-start.22 = (bf16[3,32,896]{2,1,0:T(8,128)(2,1)S(1)}, bf16[3,32,896]{2,1,0:T(8,128)(2,1)S(1)}, u32[]{:S(2)}, u32[]{:S(2)}) collective-permute-start(bf16[3,32,896]{2,1,0:T(8,128)(2,1)S(1)} %add_convert_fusion.3), channel_id=1, source_target_pairs={{0,12},{4,0},{8,4},{12,8},{1,13},{5,1},{9,5},{13,9},{2,14},{6,2},{... | collective-permute-start | bytes 516104 | tf_op jit(solution)/shard_map/ppermute | solution.py:23
  124.4 10.7 %collective-permute-start.20 = (bf16[3,32,896]{2,1,0:T(8,128)(2,1)S(1)}, bf16[3,32,896]{2,1,0:T(8,128)(2,1)S(1)}, u32[]{:S(2)}, u32[]{:S(2)}) collective-permute-start(bf16[3,32,896]{2,1,0:T(8,128)(2,1)S(1)} %add_convert_fusion.3), channel_id=1, source_target_pairs={{0,8},{4,12},{8,0},{12,4},{1,9},{5,13},{9,1},{13,5},{2,10},{6,14},... | collective-permute-start | bytes 516104 | tf_op jit(solution)/shard_map/ppermute | solution.py:23
  124.4 10.3 %collective-permute-start.21 = (bf16[3,32,896]{2,1,0:T(8,128)(2,1)S(1)}, bf16[3,32,896]{2,1,0:T(8,128)(2,1)S(1)}, u32[]{:S(2)}, u32[]{:S(2)}) collective-permute-start(bf16[3,32,896]{2,1,0:T(8,128)(2,1)S(1)} %add_convert_fusion.3), channel_id=1, source_target_pairs={{0,4},{4,8},{8,12},{12,0},{1,5},{5,9},{9,13},{13,1},{2,6},{6,10},{... | collective-permute-start | bytes 516104 | tf_op jit(solution)/shard_map/ppermute | solution.py:23
  135.3 6.2 %collective-permute-start.23 = (bf16[3,32,896]{2,1,0:T(8,128)(2,1)S(1)}, bf16[3,32,896]{2,1,0:T(8,128)(2,1)S(1)}, u32[]{:S(2)}, u32[]{:S(2)}) collective-permute-start(bf16[3,32,896]{2,1,0:T(8,128)(2,1)S(1)} %fusion.62), channel_id=1, source_target_pairs={{0,32},{1,129},{16,48},{17,145},{32,0},{33,161},{48,16},{49,177},{... | collective-permute-start | bytes 516104 | tf_op jit(solution)/shard_map/ppermute | solution.py:33
  138.1 6.2 %collective-permute-start.24 = (bf16[3,32,896]{2,1,0:T(8,128)(2,1)S(1)}, bf16[3,32,896]{2,1,0:T(8,128)(2,1)S(1)}, u32[]{:S(2)}, u32[]{:S(2)}) collective-permute-start(bf16[3,32,896]{2,1,0:T(8,128)(2,1)S(1)} %fusion.62), channel_id=1, source_target_pairs={{0,16},{1,65},{16,32},{17,81},{32,48},{33,97},{48,0},{49,113},{64,... | collective-permute-start | bytes 516104 | tf_op jit(solution)/shard_map/ppermute | solution.py:33
  144.5 7.1 %collective-permute-start.26 = (bf16[1,128,896]{2,1,0:T(8,128)(2,1)S(1)}, bf16[1,128,896]{2,1,0:T(8,128)(2,1)S(1)}, u32[]{:S(2)}, u32[]{:S(2)}) collective-permute-start(bf16[1,128,896]{2,1,0:T(8,128)(2,1)S(1)} %slice.198), channel_id=1, source_target_pairs={{0,128},{1,33},{16,144},{17,49},{32,160},{33,1},{48,176},{49,17},{... | collective-permute-start | bytes 688136 | tf_op jit(solution)/shard_map/ppermute | solution.py:33
  145.2 8.7 %collective-permute-start.27 = (bf16[1,128,896]{2,1,0:T(8,128)(2,1)S(1)}, bf16[1,128,896]{2,1,0:T(8,128)(2,1)S(1)}, u32[]{:S(2)}, u32[]{:S(2)}) collective-permute-start(bf16[1,128,896]{2,1,0:T(8,128)(2,1)S(1)} %slice.198), channel_id=1, source_target_pairs={{0,64},{1,17},{16,80},{17,33},{32,96},{33,49},{48,112},{49,1},{64,... | collective-permute-start | bytes 688136 | tf_op jit(solution)/shard_map/ppermute | solution.py:33
  146.0 7.9 %collective-permute-start.28 = (bf16[1,128,896]{2,1,0:T(8,128)(2,1)S(1)}, bf16[1,128,896]{2,1,0:T(8,128)(2,1)S(1)}, u32[]{:S(2)}, u32[]{:S(2)}) collective-permute-start(bf16[1,128,896]{2,1,0:T(8,128)(2,1)S(1)} %slice.198), channel_id=1, source_target_pairs={{0,192},{1,49},{16,208},{17,1},{32,224},{33,17},{48,240},{49,33},{... | collective-permute-start | bytes 688136 | tf_op jit(solution)/shard_map/ppermute | solution.py:33
  148.0 11.1 %collective-permute-start.29 = (bf16[2,128,896]{2,1,0:T(8,128)(2,1)S(1)}, bf16[2,128,896]{2,1,0:T(8,128)(2,1)S(1)}, u32[]{:S(2)}, u32[]{:S(2)}) collective-permute-start(bf16[2,128,896]{2,1,0:T(8,128)(2,1)S(1)} %slice.199), channel_id=1, source_target_pairs={{0,128},{1,33},{16,144},{17,49},{32,160},{33,1},{48,176},{49,17},{... | collective-permute-start | bytes 1376264 | tf_op jit(solution)/shard_map/ppermute | solution.py:33
  149.9 14.1 %collective-permute-start.30 = (bf16[2,128,896]{2,1,0:T(8,128)(2,1)S(1)}, bf16[2,128,896]{2,1,0:T(8,128)(2,1)S(1)}, u32[]{:S(2)}, u32[]{:S(2)}) collective-permute-start(bf16[2,128,896]{2,1,0:T(8,128)(2,1)S(1)} %slice.199), channel_id=1, source_target_pairs={{0,64},{1,17},{16,80},{17,33},{32,96},{33,49},{48,112},{49,1},{64,... | collective-permute-start | bytes 1376264 | tf_op jit(solution)/shard_map/ppermute | solution.py:33
  151.5 12.5 %collective-permute-start.31 = (bf16[2,128,896]{2,1,0:T(8,128)(2,1)S(1)}, bf16[2,128,896]{2,1,0:T(8,128)(2,1)S(1)}, u32[]{:S(2)}, u32[]{:S(2)}) collective-permute-start(bf16[2,128,896]{2,1,0:T(8,128)(2,1)S(1)} %slice.199), channel_id=1, source_target_pairs={{0,192},{1,49},{16,208},{17,1},{32,224},{33,17},{48,240},{49,33},{... | collective-permute-start | bytes 1376264 | tf_op jit(solution)/shard_map/ppermute | solution.py:33
  166.5 10.7 %collective-permute-start.32 = (bf16[1,256,256]{2,1,0:T(8,128)(2,1)S(1)}, bf16[1,256,256]{2,1,0:T(8,128)(2,1)S(1)}, u32[]{:S(2)}, u32[]{:S(2)}) collective-permute-start(bf16[1,256,256]{2,1,0:T(8,128)(2,1)S(1)} %bitcast.226), channel_id=1, source_target_pairs={{0,1},{1,0},{2,3},{3,2},{4,5},{5,4},{6,7},{7,6},{8,9},{9,8},{10,11... | collective-permute-start | bytes 393224 | tf_op jit(solution)/shard_map/ppermute | solution.py:37
  175.6 7.9 %collective-permute-start.35 = (bf16[2,256,256]{2,1,0:T(8,128)(2,1)S(1)}, bf16[2,256,256]{2,1,0:T(8,128)(2,1)S(1)}, u32[]{:S(2)}, u32[]{:S(2)}) collective-permute-start(bf16[2,256,256]{2,1,0:T(8,128)(2,1)S(1)} %bitcast.214), channel_id=1, source_target_pairs={{0,1},{1,0},{2,3},{3,2},{4,5},{5,4},{6,7},{7,6},{8,9},{9,8},{10,11... | collective-permute-start | bytes 786440 | tf_op jit(solution)/shard_map/ppermute | solution.py:37
  183.6 7.9 %collective-permute-start.36 = (bf16[2,256,256]{2,1,0:T(8,128)(2,1)S(1)}, bf16[2,256,256]{2,1,0:T(8,128)(2,1)S(1)}, u32[]{:S(2)}, u32[]{:S(2)}) collective-permute-start(bf16[2,256,256]{2,1,0:T(8,128)(2,1)S(1)} %fusion.30), channel_id=1, source_target_pairs={{0,2},{2,0},{1,3},{3,1},{4,6},{6,4},{5,7},{7,5},{8,10},{10,8},{9,1... | collective-permute-start | bytes 786440 | tf_op jit(solution)/shard_map/ppermute | solution.py:37
  (21 other events, 161.0 us)

commit v3 on v1

--- a/solution.py
+++ b/solution.py
@@ -110,9 +110,8 @@
 
 def on_device(acts_in, targets, enc_weight, enc_bias, dec_weight, dec_bias):
     layers = enc_weight.shape[0]
-    near = lax.optimization_barrier(spread(jnp.concatenate([acts_in, targets], axis=0), "zh"))
-    targets_near = near[layers:]
-    acts = spread_wide(lax.optimization_barrier(spread(near[:layers], "first")))
+    acts = lax.optimization_barrier(spread(lax.optimization_barrier(spread(acts_in, "zh")), "first"))
+    acts = spread_wide(acts)
     loss_scale = 1.0 / math.sqrt(acts.shape[1])
 
     partial = jnp.einsum("ltd,ldf->ltf", acts, enc_weight, preferred_element_type=F32)
@@ -128,10 +127,12 @@
                 feature[source], dec_weight[pair_index(source, target, layers)], preferred_element_type=F32
             )
         totals = lax.dynamic_update_slice(totals, total.astype(BF16)[None], (target, 0, 0))
-    part = fold(lax.optimization_barrier(fold(totals, "second")), "first")
-    recon = fold_all(part.astype(BF16))
-    near = (recon + dec_bias[:, None, :] - targets_near.astype(F32)).astype(BF16)
-    errors = near[:, : targets.shape[1]]
+    wide = lax.optimization_barrier(fold(totals, "second").astype(BF16))
+    part = fold(wide, "first")
+    rows = targets.shape[1]
+    own = part[:, :rows] + dec_bias[:, None, :] - targets.astype(F32)
+    near = fold_all(jnp.concatenate([own, part[:, rows:]], axis=1).astype(BF16)).astype(BF16)
+    errors = near[:, :rows]
     near = near + swap(near[:, :1, :1], "core") * jnp.zeros((), BF16)
     err_first = lax.optimization_barrier(spread(near, "first"))
     late = spread_wide(err_first[1:])

time: 196 us -> 193 us (0.985)
  waiting for transfers between devices: 96.2 us -> 90.9 us
  starting transfers between devices: 73.7 us -> 78.9 us
  local copies, waits for them, and re-layouts: 10.1 us -> 6.62 us
    ppermute x11, starting transfers between devices: 20.9 us -> 32.5 us  [swap(): return lax.ppermute(value, axis, [(0, 1), (1, 0)])]
    ppermute x21, starting transfers between devices: 34.8 us -> 29.7 us  [shift(): return lax.ppermute(value, ('y', 'x', 'core'), pairs)]
    ppermute x6, waiting for transfers between devices: 13.7 us -> 10.5 us  [shift(): lax.ppermute(value, 'zh', [(i, (i + by) % RING) for i in range(RING)])]
    ppermute x11, waiting for transfers between devices: 29.6 us -> 27.6 us  [swap(): return lax.ppermute(value, axis, [(0, 1), (1, 0)])]
  transfers between devices with their start and end apart: 38 -> 38, of which waited for: 29 -> 28; matrix products, arithmetic and copies ran while one was open for 4% -> 3% of each run, Pallas kernels for 0% -> 0%
where the time goes in v3:
time: 193 us
  waiting for transfers between devices  90.9 us (47%)
  starting transfers between devices  78.9 us (41%)
  matrix products  11.7 us (6%)
  local copies, waits for them, and re-layouts  6.62 us (3%)
  other arithmetic  3.38 us (2%)
    ppermute x21, waiting for transfers between devices, shift(): return lax.ppermute(value, ('y', 'x', 'core'), pairs)  52.8 us
    ppermute x11, starting transfers between devices, swap(): return lax.ppermute(value, axis, [(0, 1), (1, 0)])  32.5 us
    ppermute x21, starting transfers between devices, shift(): return lax.ppermute(value, ('y', 'x', 'core'), pairs)  29.7 us
    ppermute x11, waiting for transfers between devices, swap(): return lax.ppermute(value, axis, [(0, 1), (1, 0)])  27.6 us
    ppermute x6, starting transfers between devices, shift(): lax.ppermute(value, 'zh', [(i, (i + by) % RING) for i in range(RING)])  16.7 us
    ppermute x6, waiting for transfers between devices, shift(): lax.ppermute(value, 'zh', [(i, (i + by) % RING) for i in range(RING)])  10.5 us
  transfers between devices with their start and end apart: 38, of which 28 were waited for; matrix products, arithmetic and copies ran while one was open for 3% of the time, Pallas kernels for 0%

profile of v3, /device:TPU:1, one launch (start us, length us, event | category | flops | bytes accessed | tf_op | source)
XLA Modules:
  0.0 192.7 jit_solution(7814858871667167009)
XLA Ops:
  0.6 7.8 %collective-permute-start = (bf16[3,8,896]{2,1,0:T(8,128)(2,1)}, bf16[3,8,896]{2,1,0:T(8,128)(2,1)S(1)}, u32[]{:S(2)}, u32[]{:S(2)}) collective-permute-start(bf16[3,8,896]{2,1,0:T(8,128)(2,1)} %param.6), channel_id=1, source_target_pairs={{0,8},{4,12},{8,0},{12,4},{1,9},{5,13},{9,1},{13,5},{2,10},{6,14},... | collective-permute-start | bytes 129032 | tf_op jit(solution)/shard_map/ppermute | solution.py:23
  14.7 3.0 %collective-permute-start.3 = (bf16[3,32,896]{2,1,0:T(8,128)(2,1)S(1)}, bf16[3,32,896]{2,1,0:T(8,128)(2,1)S(1)}, u32[]{:S(2)}, u32[]{:S(2)}) collective-permute-start(bf16[3,32,896]{2,1,0:T(8,128)(2,1)S(1)} %pad_maximum_fusion.8), channel_id=1, source_target_pairs={{0,32},{1,129},{16,48},{17,145},{32,0},{33,161},{48,16},{49,177},{... | collective-permute-start | bytes 516104 | tf_op jit(solution)/shard_map/ppermute | solution.py:33
  20.5 2.9 %collective-permute-done.4 = bf16[3,32,896]{2,1,0:T(8,128)(2,1)S(1)} collective-permute-done((bf16[3,32,896]{2,1,0:T(8,128)(2,1)S(1)}, bf16[3,32,896]{2,1,0:T(8,128)(2,1)S(1)}, u32[]{:S(2)}, u32[]{:S(2)}) %collective-permute-start.4) | collective-permute-done | bytes 172064 | tf_op jit(solution)/shard_map/ppermute | solution.py:33
  23.5 2.7 %collective-permute-start.6 = (bf16[3,128,896]{2,1,0:T(8,128)(2,1)S(1)}, bf16[3,128,896]{2,1,0:T(8,128)(2,1)}, u32[]{:S(2)}, u32[]{:S(2)}) collective-permute-start(bf16[3,128,896]{2,1,0:T(8,128)(2,1)S(1)} %pad_maximum_fusion.1), channel_id=1, source_target_pairs={{0,128},{1,33},{16,144},{17,49},{32,160},{33,1},{48,176},{49,17},{... | collective-permute-start | bytes 2064392 | tf_op jit(solution)/shard_map/ppermute | solution.py:33
  29.1 6.0 %collective-permute-done.6 = bf16[3,128,896]{2,1,0:T(8,128)(2,1)} collective-permute-done((bf16[3,128,896]{2,1,0:T(8,128)(2,1)S(1)}, bf16[3,128,896]{2,1,0:T(8,128)(2,1)}, u32[]{:S(2)}, u32[]{:S(2)}) %collective-permute-start.6) | collective-permute-done | bytes 688160 | tf_op jit(solution)/shard_map/ppermute | solution.py:33
  36.3 6.4 %collective-permute-done.7 = bf16[3,128,896]{2,1,0:T(8,128)(2,1)S(1)} collective-permute-done((bf16[3,128,896]{2,1,0:T(8,128)(2,1)S(1)}, bf16[3,128,896]{2,1,0:T(8,128)(2,1)S(1)}, u32[]{:S(2)}, u32[]{:S(2)}) %collective-permute-start.7) | collective-permute-done | bytes 688160 | tf_op jit(solution)/shard_map/ppermute | solution.py:33
  45.4 10.6 %collective-permute-start.9 = (f32[3,256,256]{2,1,0:T(8,128)}, f32[3,256,256]{2,1,0:T(8,128)S(1)}, u32[]{:S(2)}, u32[]{:S(2)}) collective-permute-start(f32[3,256,256]{2,1,0:T(8,128)} %bitcast.2), channel_id=1, source_target_pairs={{0,1},{1,0},{2,3},{3,2},{4,5},{5,4},{6,7},{7,6},{8,9},{9,8},{10,11... | collective-permute-start | bytes 2359304 | tf_op jit(solution)/shard_map/ppermute | solution.py:37
  60.5 9.1 %collective-permute-done.10 = f32[3,128,256]{2,1,0:T(8,128)S(1)} collective-permute-done((f32[3,128,256]{2,1,0:T(8,128)S(1)}, f32[3,128,256]{2,1,0:T(8,128)S(1)}, u32[]{:S(2)}, u32[]{:S(2)}) %collective-permute-start.10) | collective-permute-done | bytes 393248 | tf_op jit(solution)/shard_map/ppermute | solution.py:37
  71.0 4.3 %collective-permute-done.11 = bf16[3,128,256]{2,1,0:T(8,128)(2,1)S(1)} collective-permute-done((bf16[3,128,256]{2,1,0:T(8,128)(2,1)S(1)}, bf16[3,128,256]{2,1,0:T(8,128)(2,1)S(1)}, u32[]{:S(2)}, u32[]{:S(2)}) %collective-permute-start.11) | collective-permute-done | bytes 196640 | tf_op jit(solution)/shard_map/ppermute | solution.py:37
  83.9 3.5 %collective-permute-start.13 = (bf16[3,128,896]{2,1,0:T(8,128)(2,1)S(1)}, bf16[3,128,896]{2,1,0:T(8,128)(2,1)S(1)}, u32[]{:S(2)}, u32[]{:S(2)}) collective-permute-start(bf16[3,128,896]{2,1,0:T(8,128)(2,1)S(1)} %get-tuple-element.4), channel_id=1, source_target_pairs={{0,192},{1,49},{16,208},{17,1},{32,224},{33,17},{48,240},{49,33},{... | collective-permute-start | bytes 2064392 | tf_op jit(solution)/shard_map/ppermute | solution.py:33
  88.7 14.0 %collective-permute-done.13 = bf16[3,128,896]{2,1,0:T(8,128)(2,1)S(1)} collective-permute-done((bf16[3,128,896]{2,1,0:T(8,128)(2,1)S(1)}, bf16[3,128,896]{2,1,0:T(8,128)(2,1)S(1)}, u32[]{:S(2)}, u32[]{:S(2)}) %collective-permute-start.13) | collective-permute-done | bytes 688160 | tf_op jit(solution)/shard_map/ppermute | solution.py:33
  102.7 3.1 %collective-permute-done.14 = bf16[3,128,896]{2,1,0:T(8,128)(2,1)S(1)} collective-permute-done((bf16[3,128,896]{2,1,0:T(8,128)(2,1)S(1)}, bf16[3,128,896]{2,1,0:T(8,128)(2,1)S(1)}, u32[]{:S(2)}, u32[]{:S(2)}) %collective-permute-start.14) | collective-permute-done | bytes 688160 | tf_op jit(solution)/shard_map/ppermute | solution.py:33
  112.1 2.7 %collective-permute-done.18 = bf16[3,32,896]{2,1,0:T(8,128)(2,1)S(1)} collective-permute-done((bf16[3,32,896]{2,1,0:T(8,128)(2,1)S(1)}, bf16[3,32,896]{2,1,0:T(8,128)(2,1)S(1)}, u32[]{:S(2)}, u32[]{:S(2)}) %collective-permute-start.18) | collective-permute-done | bytes 172064 | tf_op jit(solution)/shard_map/ppermute | solution.py:33
  115.0 3.1 %collective-permute-start.21 = (bf16[3,32,896]{2,1,0:T(8,128)(2,1)S(1)}, bf16[3,32,896]{2,1,0:T(8,128)(2,1)S(1)}, u32[]{:S(2)}, u32[]{:S(2)}) collective-permute-start(bf16[3,32,896]{2,1,0:T(8,128)(2,1)S(1)} %pad_maximum_fusion.9), channel_id=1, source_target_pairs={{0,12},{4,0},{8,4},{12,8},{1,13},{5,1},{9,5},{13,9},{2,14},{6,2},{... | collective-permute-start | bytes 516104 | tf_op jit(solution)/shard_map/ppermute | solution.py:23
  120.3 2.9 %collective-permute-done.21 = bf16[3,32,896]{2,1,0:T(8,128)(2,1)S(1)} collective-permute-done((bf16[3,32,896]{2,1,0:T(8,128)(2,1)S(1)}, bf16[3,32,896]{2,1,0:T(8,128)(2,1)S(1)}, u32[]{:S(2)}, u32[]{:S(2)}) %collective-permute-start.21) | collective-permute-done | bytes 172064 | tf_op jit(solution)/shard_map/ppermute | solution.py:23
  123.2 5.3 %collective-permute-done.20 = bf16[3,32,896]{2,1,0:T(8,128)(2,1)S(1)} collective-permute-done((bf16[3,32,896]{2,1,0:T(8,128)(2,1)S(1)}, bf16[3,32,896]{2,1,0:T(8,128)(2,1)S(1)}, u32[]{:S(2)}, u32[]{:S(2)}) %collective-permute-start.20) | collective-permute-done | bytes 172064 | tf_op jit(solution)/shard_map/ppermute | solution.py:23
  129.1 5.6 %collective-permute-start.22 = (bf16[3,1,1]{2,1,0:T(2,128)(2,1)S(1)}, bf16[3,1,1]{2,1,0:T(2,128)(2,1)S(1)}, u32[]{:S(2)}, u32[]{:S(2)}) collective-permute-start(bf16[3,1,1]{2,1,0:T(2,128)(2,1)S(1)} %slice.198), channel_id=1, source_target_pairs={{0,1},{1,0},{2,3},{3,2},{4,5},{5,4},{6,7},{7,6},{8,9},{9,8},{10,11... | collective-permute-start | bytes 26 | tf_op jit(solution)/shard_map/ppermute | solution.py:37
  137.3 2.7 %collective-permute-start.25 = (bf16[3,32,896]{2,1,0:T(8,128)(2,1)S(1)}, bf16[3,32,896]{2,1,0:T(8,128)(2,1)S(1)}, u32[]{:S(2)}, u32[]{:S(2)}) collective-permute-start(bf16[3,32,896]{2,1,0:T(8,128)(2,1)S(1)} %broadcast_add_fusion), channel_id=1, source_target_pairs={{0,48},{1,193},{16,0},{17,209},{32,16},{33,225},{48,32},{49,241},{... | collective-permute-start | bytes 516104 | tf_op jit(solution)/shard_map/ppermute | solution.py:33
  144.6 2.7 %collective-permute-start.28 = (bf16[1,128,896]{2,1,0:T(8,128)(2,1)S(1)}, bf16[1,128,896]{2,1,0:T(8,128)(2,1)S(1)}, u32[]{:S(2)}, u32[]{:S(2)}) collective-permute-start(bf16[1,128,896]{2,1,0:T(8,128)(2,1)S(1)} %slice.199), channel_id=1, source_target_pairs={{0,192},{1,49},{16,208},{17,1},{32,224},{33,17},{48,240},{49,33},{... | collective-permute-start | bytes 688136 | tf_op jit(solution)/shard_map/ppermute | solution.py:33
  158.1 4.8 %collective-permute-done.30 = bf16[2,128,896]{2,1,0:T(8,128)(2,1)S(1)} collective-permute-done((bf16[2,128,896]{2,1,0:T(8,128)(2,1)S(1)}, bf16[2,128,896]{2,1,0:T(8,128)(2,1)S(1)}, u32[]{:S(2)}, u32[]{:S(2)}) %collective-permute-start.30) | collective-permute-done | bytes 458784 | tf_op jit(solution)/shard_map/ppermute | solution.py:33
  165.5 3.0 %collective-permute-start.32 = (bf16[1,256,256]{2,1,0:T(8,128)(2,1)S(1)}, bf16[1,256,256]{2,1,0:T(8,128)(2,1)S(1)}, u32[]{:S(2)}, u32[]{:S(2)}) collective-permute-start(bf16[1,256,256]{2,1,0:T(8,128)(2,1)S(1)} %bitcast.225), channel_id=1, source_target_pairs={{0,1},{1,0},{2,3},{3,2},{4,5},{5,4},{6,7},{7,6},{8,9},{9,8},{10,11... | collective-permute-start | bytes 393224 | tf_op jit(solution)/shard_map/ppermute | solution.py:37
  170.8 3.9 %collective-permute-start.33 = (bf16[1,256,256]{2,1,0:T(8,128)(2,1)S(1)}, bf16[1,256,256]{2,1,0:T(8,128)(2,1)S(1)}, u32[]{:S(2)}, u32[]{:S(2)}) collective-permute-start(bf16[1,256,256]{2,1,0:T(8,128)(2,1)S(1)} %fusion.66), channel_id=1, source_target_pairs={{0,2},{2,0},{1,3},{3,1},{4,6},{6,4},{5,7},{7,5},{8,10},{10,8},{9,1... | collective-permute-start | bytes 393224 | tf_op jit(solution)/shard_map/ppermute | solution.py:37
  175.2 2.9 %collective-permute-done.33 = bf16[1,256,256]{2,1,0:T(8,128)(2,1)S(1)} collective-permute-done((bf16[1,256,256]{2,1,0:T(8,128)(2,1)S(1)}, bf16[1,256,256]{2,1,0:T(8,128)(2,1)S(1)}, u32[]{:S(2)}, u32[]{:S(2)}) %collective-permute-start.33) | collective-permute-done | bytes 131104 | tf_op jit(solution)/shard_map/ppermute | solution.py:37
  181.6 5.8 %collective-permute-done.36 = bf16[2,256,256]{2,1,0:T(8,128)(2,1)S(1)} collective-permute-done((bf16[2,256,256]{2,1,0:T(8,128)(2,1)S(1)}, bf16[2,256,256]{2,1,0:T(8,128)(2,1)S(1)}, u32[]{:S(2)}, u32[]{:S(2)}) %collective-permute-start.36) | collective-permute-done | bytes 262176 | tf_op jit(solution)/shard_map/ppermute | solution.py:37
  (153 shorter events, 72.6 us)
Async XLA Ops:
  0.6 11.4 %collective-permute-start = (bf16[3,8,896]{2,1,0:T(8,128)(2,1)}, bf16[3,8,896]{2,1,0:T(8,128)(2,1)S(1)}, u32[]{:S(2)}, u32[]{:S(2)}) collective-permute-start(bf16[3,8,896]{2,1,0:T(8,128)(2,1)} %param.6), channel_id=1, source_target_pairs={{0,8},{4,12},{8,0},{12,4},{1,9},{5,13},{9,1},{13,5},{2,10},{6,14},... | collective-permute-start | bytes 129032 | tf_op jit(solution)/shard_map/ppermute | solution.py:23
  23.5 11.6 %collective-permute-start.6 = (bf16[3,128,896]{2,1,0:T(8,128)(2,1)S(1)}, bf16[3,128,896]{2,1,0:T(8,128)(2,1)}, u32[]{:S(2)}, u32[]{:S(2)}) collective-permute-start(bf16[3,128,896]{2,1,0:T(8,128)(2,1)S(1)} %pad_maximum_fusion.1), channel_id=1, source_target_pairs={{0,128},{1,33},{16,144},{17,49},{32,160},{33,1},{48,176},{49,17},{... | collective-permute-start | bytes 2064392 | tf_op jit(solution)/shard_map/ppermute | solution.py:33
  26.2 16.5 %collective-permute-start.7 = (bf16[3,128,896]{2,1,0:T(8,128)(2,1)S(1)}, bf16[3,128,896]{2,1,0:T(8,128)(2,1)S(1)}, u32[]{:S(2)}, u32[]{:S(2)}) collective-permute-start(bf16[3,128,896]{2,1,0:T(8,128)(2,1)S(1)} %pad_maximum_fusion.1), channel_id=1, source_target_pairs={{0,64},{1,17},{16,80},{17,33},{32,96},{33,49},{48,112},{49,1},{64,... | collective-permute-start | bytes 2064392 | tf_op jit(solution)/shard_map/ppermute | solution.py:33
  26.7 16.1 %collective-permute-start.8 = (bf16[3,128,896]{2,1,0:T(8,128)(2,1)S(1)}, bf16[3,128,896]{2,1,0:T(8,128)(2,1)S(1)}, u32[]{:S(2)}, u32[]{:S(2)}) collective-permute-start(bf16[3,128,896]{2,1,0:T(8,128)(2,1)S(1)} %pad_maximum_fusion.1), channel_id=1, source_target_pairs={{0,192},{1,49},{16,208},{17,1},{32,224},{33,17},{48,240},{49,33},{... | collective-permute-start | bytes 2064392 | tf_op jit(solution)/shard_map/ppermute | solution.py:33
  45.4 12.7 %collective-permute-start.9 = (f32[3,256,256]{2,1,0:T(8,128)}, f32[3,256,256]{2,1,0:T(8,128)S(1)}, u32[]{:S(2)}, u32[]{:S(2)}) collective-permute-start(f32[3,256,256]{2,1,0:T(8,128)} %bitcast.2), channel_id=1, source_target_pairs={{0,1},{1,0},{2,3},{3,2},{4,5},{5,4},{6,7},{7,6},{8,9},{9,8},{10,11... | collective-permute-start | bytes 2359304 | tf_op jit(solution)/shard_map/ppermute | solution.py:37
  58.3 11.3 %collective-permute-start.10 = (f32[3,128,256]{2,1,0:T(8,128)S(1)}, f32[3,128,256]{2,1,0:T(8,128)S(1)}, u32[]{:S(2)}, u32[]{:S(2)}) collective-permute-start(f32[3,128,256]{2,1,0:T(8,128)S(1)} %constant_dynamic-slice_fusion.2), channel_id=1, source_target_pairs={{0,2},{2,0},{1,3},{3,1},{4,6},{6,4},{5,7},{7,5},{8,10},{10,8},{9,1... | collective-permute-start | bytes 1179656 | tf_op jit(solution)/shard_map/ppermute | solution.py:37
  83.9 18.7 %collective-permute-start.13 = (bf16[3,128,896]{2,1,0:T(8,128)(2,1)S(1)}, bf16[3,128,896]{2,1,0:T(8,128)(2,1)S(1)}, u32[]{:S(2)}, u32[]{:S(2)}) collective-permute-start(bf16[3,128,896]{2,1,0:T(8,128)(2,1)S(1)} %get-tuple-element.4), channel_id=1, source_target_pairs={{0,192},{1,49},{16,208},{17,1},{32,224},{33,17},{48,240},{49,33},{... | collective-permute-start | bytes 2064392 | tf_op jit(solution)/shard_map/ppermute | solution.py:33
  87.4 18.4 %collective-permute-start.14 = (bf16[3,128,896]{2,1,0:T(8,128)(2,1)S(1)}, bf16[3,128,896]{2,1,0:T(8,128)(2,1)S(1)}, u32[]{:S(2)}, u32[]{:S(2)}) collective-permute-start(bf16[3,128,896]{2,1,0:T(8,128)(2,1)S(1)} %get-tuple-element.6), channel_id=1, source_target_pairs={{0,64},{1,17},{16,80},{17,33},{32,96},{33,49},{48,112},{49,1},{64,... | collective-permute-start | bytes 2064392 | tf_op jit(solution)/shard_map/ppermute | solution.py:33
  87.4 18.4 %collective-permute-start.15 = (bf16[3,128,896]{2,1,0:T(8,128)(2,1)S(1)}, bf16[3,128,896]{2,1,0:T(8,128)(2,1)S(1)}, u32[]{:S(2)}, u32[]{:S(2)}) collective-permute-start(bf16[3,128,896]{2,1,0:T(8,128)(2,1)S(1)} %get-tuple-element.5), channel_id=1, source_target_pairs={{0,128},{1,33},{16,144},{17,49},{32,160},{33,1},{48,176},{49,17},{... | collective-permute-start | bytes 2064392 | tf_op jit(solution)/shard_map/ppermute | solution.py:33
  108.2 6.6 %collective-permute-start.18 = (bf16[3,32,896]{2,1,0:T(8,128)(2,1)S(1)}, bf16[3,32,896]{2,1,0:T(8,128)(2,1)S(1)}, u32[]{:S(2)}, u32[]{:S(2)}) collective-permute-start(bf16[3,32,896]{2,1,0:T(8,128)(2,1)S(1)} %get-tuple-element.15), channel_id=1, source_target_pairs={{0,32},{1,129},{16,48},{17,145},{32,0},{33,161},{48,16},{49,177},{... | collective-permute-start | bytes 516104 | tf_op jit(solution)/shard_map/ppermute | solution.py:33
  115.0 8.2 %collective-permute-start.21 = (bf16[3,32,896]{2,1,0:T(8,128)(2,1)S(1)}, bf16[3,32,896]{2,1,0:T(8,128)(2,1)S(1)}, u32[]{:S(2)}, u32[]{:S(2)}) collective-permute-start(bf16[3,32,896]{2,1,0:T(8,128)(2,1)S(1)} %pad_maximum_fusion.9), channel_id=1, source_target_pairs={{0,12},{4,0},{8,4},{12,8},{1,13},{5,1},{9,5},{13,9},{2,14},{6,2},{... | collective-permute-start | bytes 516104 | tf_op jit(solution)/shard_map/ppermute | solution.py:23
  118.1 10.9 %collective-permute-start.19 = (bf16[3,32,896]{2,1,0:T(8,128)(2,1)S(1)}, bf16[3,32,896]{2,1,0:T(8,128)(2,1)S(1)}, u32[]{:S(2)}, u32[]{:S(2)}) collective-permute-start(bf16[3,32,896]{2,1,0:T(8,128)(2,1)S(1)} %pad_maximum_fusion.9), channel_id=1, source_target_pairs={{0,8},{4,12},{8,0},{12,4},{1,9},{5,13},{9,1},{13,5},{2,10},{6,14},... | collective-permute-start | bytes 516104 | tf_op jit(solution)/shard_map/ppermute | solution.py:23
  118.9 9.6 %collective-permute-start.20 = (bf16[3,32,896]{2,1,0:T(8,128)(2,1)S(1)}, bf16[3,32,896]{2,1,0:T(8,128)(2,1)S(1)}, u32[]{:S(2)}, u32[]{:S(2)}) collective-permute-start(bf16[3,32,896]{2,1,0:T(8,128)(2,1)S(1)} %pad_maximum_fusion.9), channel_id=1, source_target_pairs={{0,4},{4,8},{8,12},{12,0},{1,5},{5,9},{9,13},{13,1},{2,6},{6,10},{... | collective-permute-start | bytes 516104 | tf_op jit(solution)/shard_map/ppermute | solution.py:23
  129.1 6.5 %collective-permute-start.22 = (bf16[3,1,1]{2,1,0:T(2,128)(2,1)S(1)}, bf16[3,1,1]{2,1,0:T(2,128)(2,1)S(1)}, u32[]{:S(2)}, u32[]{:S(2)}) collective-permute-start(bf16[3,1,1]{2,1,0:T(2,128)(2,1)S(1)} %slice.198), channel_id=1, source_target_pairs={{0,1},{1,0},{2,3},{3,2},{4,5},{5,4},{6,7},{7,6},{8,9},{9,8},{10,11... | collective-permute-start | bytes 26 | tf_op jit(solution)/shard_map/ppermute | solution.py:37
  137.3 6.4 %collective-permute-start.25 = (bf16[3,32,896]{2,1,0:T(8,128)(2,1)S(1)}, bf16[3,32,896]{2,1,0:T(8,128)(2,1)S(1)}, u32[]{:S(2)}, u32[]{:S(2)}) collective-permute-start(bf16[3,32,896]{2,1,0:T(8,128)(2,1)S(1)} %broadcast_add_fusion), channel_id=1, source_target_pairs={{0,48},{1,193},{16,0},{17,209},{32,16},{33,225},{48,32},{49,241},{... | collective-permute-start | bytes 516104 | tf_op jit(solution)/shard_map/ppermute | solution.py:33
  143.9 6.8 %collective-permute-start.26 = (bf16[1,128,896]{2,1,0:T(8,128)(2,1)S(1)}, bf16[1,128,896]{2,1,0:T(8,128)(2,1)S(1)}, u32[]{:S(2)}, u32[]{:S(2)}) collective-permute-start(bf16[1,128,896]{2,1,0:T(8,128)(2,1)S(1)} %slice.199), channel_id=1, source_target_pairs={{0,128},{1,33},{16,144},{17,49},{32,160},{33,1},{48,176},{49,17},{... | collective-permute-start | bytes 688136 | tf_op jit(solution)/shard_map/ppermute | solution.py:33
  144.6 8.5 %collective-permute-start.27 = (bf16[1,128,896]{2,1,0:T(8,128)(2,1)S(1)}, bf16[1,128,896]{2,1,0:T(8,128)(2,1)S(1)}, u32[]{:S(2)}, u32[]{:S(2)}) collective-permute-start(bf16[1,128,896]{2,1,0:T(8,128)(2,1)S(1)} %slice.199), channel_id=1, source_target_pairs={{0,64},{1,17},{16,80},{17,33},{32,96},{33,49},{48,112},{49,1},{64,... | collective-permute-start | bytes 688136 | tf_op jit(solution)/shard_map/ppermute | solution.py:33
  144.6 10.6 %collective-permute-start.28 = (bf16[1,128,896]{2,1,0:T(8,128)(2,1)S(1)}, bf16[1,128,896]{2,1,0:T(8,128)(2,1)S(1)}, u32[]{:S(2)}, u32[]{:S(2)}) collective-permute-start(bf16[1,128,896]{2,1,0:T(8,128)(2,1)S(1)} %slice.199), channel_id=1, source_target_pairs={{0,192},{1,49},{16,208},{17,1},{32,224},{33,17},{48,240},{49,33},{... | collective-permute-start | bytes 688136 | tf_op jit(solution)/shard_map/ppermute | solution.py:33
  147.5 10.6 %collective-permute-start.29 = (bf16[2,128,896]{2,1,0:T(8,128)(2,1)S(1)}, bf16[2,128,896]{2,1,0:T(8,128)(2,1)S(1)}, u32[]{:S(2)}, u32[]{:S(2)}) collective-permute-start(bf16[2,128,896]{2,1,0:T(8,128)(2,1)S(1)} %slice.200), channel_id=1, source_target_pairs={{0,128},{1,33},{16,144},{17,49},{32,160},{33,1},{48,176},{49,17},{... | collective-permute-start | bytes 1376264 | tf_op jit(solution)/shard_map/ppermute | solution.py:33
  149.3 13.7 %collective-permute-start.30 = (bf16[2,128,896]{2,1,0:T(8,128)(2,1)S(1)}, bf16[2,128,896]{2,1,0:T(8,128)(2,1)S(1)}, u32[]{:S(2)}, u32[]{:S(2)}) collective-permute-start(bf16[2,128,896]{2,1,0:T(8,128)(2,1)S(1)} %slice.200), channel_id=1, source_target_pairs={{0,64},{1,17},{16,80},{17,33},{32,96},{33,49},{48,112},{49,1},{64,... | collective-permute-start | bytes 1376264 | tf_op jit(solution)/shard_map/ppermute | solution.py:33
  150.7 12.3 %collective-permute-start.31 = (bf16[2,128,896]{2,1,0:T(8,128)(2,1)S(1)}, bf16[2,128,896]{2,1,0:T(8,128)(2,1)S(1)}, u32[]{:S(2)}, u32[]{:S(2)}) collective-permute-start(bf16[2,128,896]{2,1,0:T(8,128)(2,1)S(1)} %slice.200), channel_id=1, source_target_pairs={{0,192},{1,49},{16,208},{17,1},{32,224},{33,17},{48,240},{49,33},{... | collective-permute-start | bytes 1376264 | tf_op jit(solution)/shard_map/ppermute | solution.py:33
  169.1 10.2 %collective-permute-start.35 = (bf16[2,256,256]{2,1,0:T(8,128)(2,1)S(1)}, bf16[2,256,256]{2,1,0:T(8,128)(2,1)S(1)}, u32[]{:S(2)}, u32[]{:S(2)}) collective-permute-start(bf16[2,256,256]{2,1,0:T(8,128)(2,1)S(1)} %bitcast.213), channel_id=1, source_target_pairs={{0,1},{1,0},{2,3},{3,2},{4,5},{5,4},{6,7},{7,6},{8,9},{9,8},{10,11... | collective-permute-start | bytes 786440 | tf_op jit(solution)/shard_map/ppermute | solution.py:37
  170.8 7.3 %collective-permute-start.33 = (bf16[1,256,256]{2,1,0:T(8,128)(2,1)S(1)}, bf16[1,256,256]{2,1,0:T(8,128)(2,1)S(1)}, u32[]{:S(2)}, u32[]{:S(2)}) collective-permute-start(bf16[1,256,256]{2,1,0:T(8,128)(2,1)S(1)} %fusion.66), channel_id=1, source_target_pairs={{0,2},{2,0},{1,3},{3,1},{4,6},{6,4},{5,7},{7,5},{8,10},{10,8},{9,1... | collective-permute-start | bytes 393224 | tf_op jit(solution)/shard_map/ppermute | solution.py:37
  179.5 7.9 %collective-permute-start.36 = (bf16[2,256,256]{2,1,0:T(8,128)(2,1)S(1)}, bf16[2,256,256]{2,1,0:T(8,128)(2,1)S(1)}, u32[]{:S(2)}, u32[]{:S(2)}) collective-permute-start(bf16[2,256,256]{2,1,0:T(8,128)(2,1)S(1)} %fusion.30), channel_id=1, source_target_pairs={{0,2},{2,0},{1,3},{3,1},{4,6},{6,4},{5,7},{7,5},{8,10},{10,8},{9,1... | collective-permute-start | bytes 786440 | tf_op jit(solution)/shard_map/ppermute | solution.py:37
  (22 other events, 153.8 us)
